TPU v7x, 512 devices: a whole 4x8x8 slice. The times are simulated.
512 devices in a mesh: dp: 2 (over y_lo), row: 8 (over y_hi, core), col: 32 (over z, x).
Axes of the slice: x: 4, y: 8 (y_hi: 4, y_lo: 2; y = y_hi * 2 + y_lo), z: 8, core: 2. Of those that a mesh axis runs over, the one named last changes fastest.
Arguments:
- gate_pre: bfloat16 [2048, 28672], P(('dp', 'row'), 'col'), may hold values from -6 to 6
- up_pre: bfloat16 [2048, 28672], P(('dp', 'row'), 'col'), may hold values from -6 to 6
- grad_out: bfloat16 [2048, 16384], P('col', ('dp', 'row')), may hold values from -6 to 6
- down_weight: bfloat16 [28672, 16384], P('col', ('dp', 'row')), may hold values from -0.046875 to 0.046875
- basis: bfloat16 [512, 28672], P(('dp', 'row'), 'col'), may hold values from -0.0625 to 0.0625
- first_moment_in: float32 [512, 16384], P('col', ('dp', 'row')), may hold values from -6 to 6
- second_moment_in: float32 [512, 16384], P('col', ('dp', 'row')), may hold values from 0.1 to 10
Outputs:
- grad_gate: bfloat16 [2048, 28672], P(('dp', 'row'), 'col')
- grad_up: bfloat16 [2048, 28672], P(('dp', 'row'), 'col')
- scaled_grad: bfloat16 [28672, 16384], P('col', ('dp', 'row'))
- first_moment: float32 [512, 16384], P('col', ('dp', 'row'))
- second_moment: float32 [512, 16384], P('col', ('dp', 'row'))
All inputs are finite; a program needn't handle non-finite values.
Results may differ from a plain program's by a relative error of at most 0.024.
Values may be sent and summed in bfloat16 or wider, within the bound.
No kernel may reach another device: no remote copies, remote signals or barrier semaphores. Data moves between devices by JAX's collectives and lax.ppermute only.
A program may use at most 64 MiB of HBM per device.

v0:
```python
import math

import jax
import jax.numpy as jnp
from jax import lax
from jax.experimental import pallas as pl
from jax.experimental.pallas import tpu as pltpu
from jax.sharding import PartitionSpec as P


first_fix = 1.0 - math.exp(1000.0 * math.log(0.9))
second_fix = 1.0 - math.exp(1000.0 * math.log(0.999))

BF = jnp.bfloat16
F32 = jnp.float32
TOK = ("dp", "row")
Z_GROUPS = [[4 * z + x for z in range(8)] for x in range(4)]
Y_GROUPS = [[2 * m + q for m in range(8)] for q in range(2)]
PAIR = [(k, k ^ 1) for k in range(16)]


def along_x(value):
    def target(row, c):
        return row, c - c % 4 + (c + 1 - 2 * (row % 2)) % 4

    moves = [(32 * row + c, target(row, c)) for row in range(8) for c in range(32)]
    return lax.ppermute(value, ("row", "col"), [(source, 32 * row + c) for source, (row, c) in moves])


def along_y(value):
    def index(y, core):
        return 2 * (4 * (y % 2) + y // 2) + core

    return lax.ppermute(value, TOK, [(index(y, q), index((y + 1 - 2 * q) % 8, q)) for y in range(8) for q in range(2)])


def activation(gate_pre, up_pre):
    gate_f = gate_pre.astype(F32)
    sigma = jax.nn.sigmoid(gate_f)
    return gate_f, sigma, gate_f * sigma, up_pre.astype(F32)


def dot_nt(left, right):
    return lax.dot_general(left, right, (((1,), (1,)), ((), ())), preferred_element_type=F32)


def dot_tn(left, right):
    return lax.dot_general(left, right, (((0,), (0,)), ((), ())), preferred_element_type=F32)


def place_out_kernel(here_ref, *refs):
    pieces, (own, other) = refs[:-2], refs[-2:]
    x, core = here_ref[0], here_ref[1]
    for step, piece in enumerate(pieces):
        source = lax.rem(x + 4 + step * (2 * core - 1), 4)
        mine = source // 2 == core

        @pl.when(mine)
        def _():
            own[:, source % 2] = piece[...]

        @pl.when(jnp.logical_not(mine))
        def _():
            other[:, source % 2] = piece[...]


def place_out(where, pieces):
    planes, rows, width = pieces[0].shape
    return pl.pallas_call(
        place_out_kernel,
        out_shape=[jax.ShapeDtypeStruct((planes, 2, rows, width), BF)] * 2,
        in_specs=[pl.BlockSpec(memory_space=pltpu.SMEM)] + [pl.BlockSpec(memory_space=pltpu.VMEM)] * 4,
        out_specs=[pl.BlockSpec(memory_space=pltpu.VMEM)] * 2,
        name="place_out",
    )(where, *pieces)


def place_hid_kernel(here_ref, *refs):
    pieces, out = refs[:-1], refs[-1]
    y, core = here_ref[0], here_ref[1]
    for step, piece in enumerate(pieces):
        source = lax.rem(y + 8 + step * (2 * core - 1), 8)
        out[4 * (source % 2) + source // 2] = piece[...]


def place_hid(where, pieces):
    rows, units = pieces[0].shape
    return pl.pallas_call(
        place_hid_kernel,
        out_shape=jax.ShapeDtypeStruct((8, rows, units), BF),
        in_specs=[pl.BlockSpec(memory_space=pltpu.SMEM)] + [pl.BlockSpec(memory_space=pltpu.VMEM)] * 8,
        out_specs=pl.BlockSpec(memory_space=pltpu.VMEM),
        name="place_hid",
    )(where, *pieces)


def gather_out(value, where):
    sent = jnp.broadcast_to(value[None], (8,) + value.shape).reshape((-1,) + value.shape[1:])
    got = lax.all_to_all(sent, "col", 0, 0, tiled=True, axis_index_groups=Z_GROUPS)
    pieces = [got.reshape((8,) + value.shape)]
    for _ in range(1, 4):
        pieces.append(along_x(pieces[-1]))
    return place_out(where, pieces)


def gather_hid(value, where):
    pieces = [value]
    for _ in range(1, 8):
        pieces.append(along_y(pieces[-1]))
    return place_hid(where, pieces)


def exact(left, right):
    high = left.astype(BF)
    rest = left - high.astype(F32)
    mid = rest.astype(BF)
    low = (rest - mid.astype(F32)).astype(BF)
    terms = lax.dot_general(
        jnp.concatenate([high, mid, low], axis=0), right, (((1,), (0,)), ((), ())), preferred_element_type=F32
    ).reshape(3, 16, right.shape[1])
    return terms[0] + (terms[1] + terms[2])


def work(gate_pre, up_pre, grad_out, down_weight, basis, first_moment_in, second_moment_in):
    width = grad_out.shape[1]
    units = gate_pre.shape[1]
    core = lax.axis_index("row") % 2
    y = 2 * (lax.axis_index("row") // 2) + lax.axis_index("dp")
    x = lax.axis_index("col") % 4

    out_own, out_other = gather_out(grad_out, jnp.stack([x, core]))
    out_own, out_other = out_own.reshape(1024, width), out_other.reshape(1024, width)

    _, _, act_early, up_early = activation(gate_pre, up_pre)
    hidden = (act_early * up_early).astype(BF)
    hidden_own = gather_hid(hidden, jnp.stack([y, core])).reshape(1024, units)
    hidden_other = lax.ppermute(hidden_own, TOK, PAIR)

    basis_all = lax.all_gather(basis, TOK, axis=0, tiled=True)
    tp_part = dot_nt(basis_all, hidden).astype(BF)
    tp_got = lax.all_to_all(tp_part, "col", 0, 0, tiled=True).reshape(32, 16, 128)
    tp_mine = jnp.sum(tp_got.astype(F32), axis=0)
    tp_sent = jnp.broadcast_to(tp_mine[None], (16, 16, 128)).reshape(256, 128)
    tp_all = lax.all_to_all(tp_sent, TOK, 0, 0, tiled=True).reshape(8, 2, 16, 128)

    def tp_rows(which):
        return lax.dynamic_index_in_dim(tp_all, which, 1, keepdims=False).transpose(1, 0, 2).reshape(16, 1024)

    part_other = dot_nt(out_other, down_weight).astype(BF)
    part_got = lax.ppermute(part_other, TOK, PAIR)
    part_sum = (dot_nt(out_own, down_weight) + part_got.astype(F32)).astype(BF)
    blocks = lax.all_to_all(part_sum, TOK, 0, 0, tiled=True, axis_index_groups=Y_GROUPS)
    summed = jnp.sum(blocks.reshape(8, 128, units).astype(F32), axis=0).astype(BF)
    gate_late, up_late, summed = lax.optimization_barrier((gate_pre, up_pre, summed))
    gate_f, sigma, act_value, up_f = activation(gate_late, up_late)
    grad_hidden = summed.astype(F32)
    grad_up = (grad_hidden * act_value).astype(BF)
    grad_gate = (grad_hidden * up_f * sigma * (1.0 + gate_f * (1.0 - sigma))).astype(BF)

    projected = exact(tp_rows(core), out_own) + exact(tp_rows(1 - core), out_other)
    first_moment = 0.9 * first_moment_in + 0.1 * projected
    second_moment = 0.999 * second_moment_in + 0.001 * projected * projected
    adapted = first_moment / first_fix / (jnp.sqrt(second_moment / second_fix) + 1e-06)
    totals = jnp.stack([jnp.sum(adapted * adapted, axis=0), jnp.sum(projected * projected, axis=0)])
    for bit in (1, 2, 4, 8, 16):
        totals = totals + lax.ppermute(totals, "col", [(c, c ^ bit) for c in range(32)])
    column_scale = jnp.sqrt(totals[0]) / (jnp.sqrt(totals[1]) + 1e-06)

    terms = (dot_tn(hidden_own, out_own), dot_tn(hidden_other, out_other))
    grad_weight = sum(terms).astype(BF)
    scaled_grad = (grad_weight.astype(F32) * column_scale[None, :]).astype(BF)
    return (grad_gate, grad_up, scaled_grad, first_moment, second_moment)


def solution(mesh):
    rows = P(TOK, "col")
    cols = P("col", TOK)
    return jax.shard_map(
        work,
        mesh=mesh,
        in_specs=(rows, rows, cols, cols, rows, cols, cols),
        out_specs=(rows, rows, cols, cols, cols),
        check_vma=False,
    )
```

profile of v0, /device:TPU:8, one launch (start us, length us, event | category | flops | bytes accessed | tf_op | source)
XLA Modules:
  0.0 245.7 jit_solution(5538487697437354409)
XLA Ops:
  1.8 38.8 %all_to_all.30.refs_0_ = bf16[8,64,1024]{2,1,0:T(8,128)(2,1)S(1)} all-to-all(bf16[8,64,1024]{2,1,0:T(8,128)(2,1)S(1)} %broadcast_in_dim.4), channel_id=1, replica_groups={{0,4,8,12,16,20,24,28},{1,5,9,13,17,21,25,29},{2,6,10,14,18,22,26,30},{..., dimensions={0} | all-to-all | bytes 2097152 | tf_op jit(solution)/shard_map/all_to_all | solution.py:99
  40.7 3.4 %collective-permute-start = (bf16[8,64,1024]{2,1,0:T(8,128)(2,1)S(1)}, bf16[8,64,1024]{2,1,0:T(8,128)(2,1)S(1)}, u32[]{:S(2)}, u32[]{:S(2)}) collective-permute-start(bf16[8,64,1024]{2,1,0:T(8,128)(2,1)S(1)} %all_to_all.30.refs_0_), channel_id=1, source_target_pairs={{0,1},{1,2},{2,3},{3,0},{4,5},{5,6},{6,7},{7,4},{8,9},{9,10},{10,1... | collective-permute-start | bytes 3145736 | tf_op jit(solution)/shard_map/ppermute | solution.py:27
  44.1 14.5 %collective-permute-done.refs_1_ = bf16[8,64,1024]{2,1,0:T(8,128)(2,1)S(1)} collective-permute-done((bf16[8,64,1024]{2,1,0:T(8,128)(2,1)S(1)}, bf16[8,64,1024]{2,1,0:T(8,128)(2,1)S(1)}, u32[]{:S(2)}, u32[]{:S(2)}) %collective-permute-start) | collective-permute-done | bytes 1048608 | tf_op jit(solution)/shard_map/ppermute | solution.py:27
  60.8 15.8 %collective-permute-done.1.refs_2_ = bf16[8,64,1024]{2,1,0:T(8,128)(2,1)} collective-permute-done((bf16[8,64,1024]{2,1,0:T(8,128)(2,1)S(1)}, bf16[8,64,1024]{2,1,0:T(8,128)(2,1)}, u32[]{:S(2)}, u32[]{:S(2)}) %collective-permute-start.1) | collective-permute-done | bytes 1048608 | tf_op jit(solution)/shard_map/ppermute | solution.py:27
  78.7 3.5 %collective-permute-start.4 = (bf16[128,896]{1,0:T(8,128)(2,1)S(1)}, bf16[128,896]{1,0:T(8,128)(2,1)}, u32[]{:S(2)}, u32[]{:S(2)}) collective-permute-start(bf16[128,896]{1,0:T(8,128)(2,1)S(1)} %fusion.13.refs_0_), channel_id=1, source_target_pairs={{0,256},{32,480},{256,64},{288,32},{64,320},{96,288},{320,128},{35... | collective-permute-start | bytes 688136 | tf_op jit(solution)/shard_map/ppermute | solution.py:34
  82.8 12.0 %collective-permute-done.2.refs_3_ = bf16[8,64,1024]{2,1,0:T(8,128)(2,1)} collective-permute-done((bf16[8,64,1024]{2,1,0:T(8,128)(2,1)}, bf16[8,64,1024]{2,1,0:T(8,128)(2,1)}, u32[]{:S(2)}, u32[]{:S(2)}) %collective-permute-start.2) | collective-permute-done | bytes 1048608 | tf_op jit(solution)/shard_map/ppermute | solution.py:27
  94.8 4.5 %place_out.1 = (bf16[8,2,64,1024]{3,2,1,0:T(8,128)(2,1)}, bf16[8,2,64,1024]{3,2,1,0:T(8,128)(2,1)}) custom-call(s32[2]{0:T(128)} %pad_add_fusion.here_ref, bf16[8,64,1024]{2,1,0:T(8,128)(2,1)} %copy-done.1, bf16[8,64,1024]{2,1,0:T(8,128)(2,1)} %copy-done.6, bf16[8,64,1024]{2,1,0:T(8,128)(2,1)} %collective-permute-done.1.refs_2_, ...), custom_call_target="tpu_custom_call" | custom-call | tf_op jit(solution)/shard_map/place_out/pallas_call | solution.py:69
  99.3 5.2 %convolution_convert_fusion = bf16[1024,896]{1,0:T(8,128)(2,1)} fusion(bf16[1024,1024]{1,0:T(8,128)(2,1)} %bitcast.65, bf16[896,1024]{1,0:T(8,128)(2,1)S(1)} %copy-done), kind=kOutput, calls=%fused_computation.3 | convolution fusion | flops 1879965696 | bytes 5767168 | tf_op jit(solution)/shard_map/dot_general | solution.py:44
  106.4 3.5 %collective-permute-start.5 = (bf16[128,896]{1,0:T(8,128)(2,1)}, bf16[128,896]{1,0:T(8,128)(2,1)S(1)}, u32[]{:S(2)}, u32[]{:S(2)}) collective-permute-start(bf16[128,896]{1,0:T(8,128)(2,1)} %collective-permute-done.4.refs_1_), channel_id=1, source_target_pairs={{0,256},{32,480},{256,64},{288,32},{64,320},{96,288},{320,128},{35... | collective-permute-start | bytes 688136 | tf_op jit(solution)/shard_map/ppermute | solution.py:34
  109.9 4.6 %collective-permute-done.5.refs_2_ = bf16[128,896]{1,0:T(8,128)(2,1)S(1)} collective-permute-done((bf16[128,896]{1,0:T(8,128)(2,1)}, bf16[128,896]{1,0:T(8,128)(2,1)S(1)}, u32[]{:S(2)}, u32[]{:S(2)}) %collective-permute-start.5) | collective-permute-done | bytes 229408 | tf_op jit(solution)/shard_map/ppermute | solution.py:34
  114.6 3.5 %collective-permute-start.6 = (bf16[128,896]{1,0:T(8,128)(2,1)S(1)}, bf16[128,896]{1,0:T(8,128)(2,1)S(1)}, u32[]{:S(2)}, u32[]{:S(2)}) collective-permute-start(bf16[128,896]{1,0:T(8,128)(2,1)S(1)} %collective-permute-done.5.refs_2_), channel_id=1, source_target_pairs={{0,256},{32,480},{256,64},{288,32},{64,320},{96,288},{320,128},{35... | collective-permute-start | bytes 688136 | tf_op jit(solution)/shard_map/ppermute | solution.py:34
  118.0 25.7 %all_gather.3 = bf16[512,896]{1,0:T(8,128)(2,1)S(1)} all-gather(bf16[32,896]{1,0:T(8,128)(2,1)S(1)} %copy-done.16), channel_id=1, replica_groups=mesh['dp'=2,'row'=8,'col'=32] {'dp','row'}, dimensions={0}, use_global_device_ids=true | all-gather | bytes 974848 | tf_op jit(solution)/shard_map/all_gather | solution.py:139
  143.8 4.1 %collective-permute-start.7 = (bf16[128,896]{1,0:T(8,128)(2,1)S(1)}, bf16[128,896]{1,0:T(8,128)(2,1)S(1)}, u32[]{:S(2)}, u32[]{:S(2)}) collective-permute-start(bf16[128,896]{1,0:T(8,128)(2,1)S(1)} %collective-permute-done.6.refs_3_), channel_id=1, source_target_pairs={{0,256},{32,480},{256,64},{288,32},{64,320},{96,288},{320,128},{35... | collective-permute-start | bytes 688136 | tf_op jit(solution)/shard_map/ppermute | solution.py:34
  149.1 3.8 %all-to-all-start.2 = ((bf16[32,16,128]{2,1,0:T(8,128)(2,1)}), bf16[32,16,128]{2,1,0:T(8,128)(2,1)S(1)}, u32[]{:S(2)}, u32[]{:S(2)}) async-start(bf16[32,16,128]{2,1,0:T(8,128)(2,1)} %bitcast.8), calls=%async_computation.2 | async-start | bytes 262144 | tf_op jit(solution)/shard_map/all_to_all | solution.py:141
  156.4 4.5 %collective-permute-done.8.refs_5_ = bf16[128,896]{1,0:T(8,128)(2,1)S(1)} collective-permute-done((bf16[128,896]{1,0:T(8,128)(2,1)S(1)}, bf16[128,896]{1,0:T(8,128)(2,1)S(1)}, u32[]{:S(2)}, u32[]{:S(2)}) %collective-permute-start.8) | collective-permute-done | bytes 229408 | tf_op jit(solution)/shard_map/ppermute | solution.py:34
  165.0 5.9 %all-to-all-start.3 = ((f32[16,16,128]{2,1,0:T(8,128)}), f32[16,16,128]{2,1,0:T(8,128)S(1)}, u32[]{:S(2)}, u32[]{:S(2)}) async-start(f32[16,16,128]{2,1,0:T(8,128)} %broadcast_in_dim.5), calls=%async_computation.3 | async-start | bytes 262144 | tf_op jit(solution)/shard_map/all_to_all | solution.py:144
  174.9 3.5 %all-to-all-done.3 = f32[16,16,128]{2,1,0:T(8,128)S(1)} async-done(((f32[16,16,128]{2,1,0:T(8,128)}), f32[16,16,128]{2,1,0:T(8,128)S(1)}, u32[]{:S(2)}, u32[]{:S(2)}) %all-to-all-start.3) | async-done | bytes 131104 | tf_op jit(solution)/shard_map/all_to_all | solution.py:144
  184.4 5.8 %add_convert_fusion.1 = bf16[1024,896]{1,0:T(8,128)(2,1)} fusion(bf16[1024,896]{1,0:T(8,128)(2,1)} %collective-permute-done.3, bf16[1024,1024]{1,0:T(8,128)(2,1)} %bitcast.62, bf16[896,1024]{1,0:T(8,128)(2,1)S(1)} %copy-done), kind=kOutput, calls=%fused_computation.2 | convolution fusion | flops 1881800704 | bytes 7602176 | tf_op jit(solution)/shard_map/dot_general | solution.py:44
  190.2 8.1 %all-to-all-start.1 = ((bf16[8,128,896]{2,1,0:T(8,128)(2,1)}), bf16[8,128,896]{2,1,0:T(8,128)(2,1)}, u32[]{:S(2)}, u32[]{:S(2)}) async-start(bf16[8,128,896]{2,1,0:T(8,128)(2,1)} %bitcast.68), calls=%async_computation.1 | async-start | bytes 3670016 | tf_op jit(solution)/shard_map/all_to_all | solution.py:152
  207.4 4.1 %collective-permute-start.13 = (f32[2,1024]{1,0:T(2,128)S(1)}, f32[2,1024]{1,0:T(2,128)S(1)}, u32[]{:S(2)}, u32[]{:S(2)}) collective-permute-start(f32[2,1024]{1,0:T(2,128)S(1)} %fusion.36), channel_id=1, source_target_pairs={{0,2},{1,3},{2,0},{3,1},{4,6},{5,7},{6,4},{7,5},{8,10},{9,11},{10,... | collective-permute-start | bytes 24584 | tf_op jit(solution)/shard_map/ppermute | solution.py:166
  220.1 3.5 %collective-permute-start.15 = (f32[2,1024]{1,0:T(2,128)S(1)}, f32[2,1024]{1,0:T(2,128)S(1)}, u32[]{:S(2)}, u32[]{:S(2)}) collective-permute-start(f32[2,1024]{1,0:T(2,128)S(1)} %add.104), channel_id=1, source_target_pairs={{0,8},{1,9},{2,10},{3,11},{4,12},{5,13},{6,14},{7,15},{8,0},{9,1},... | collective-permute-start | bytes 24584 | tf_op jit(solution)/shard_map/ppermute | solution.py:166
  226.5 6.9 %collective-permute-start.16 = (f32[2,1024]{1,0:T(2,128)S(1)}, f32[2,1024]{1,0:T(2,128)S(1)}, u32[]{:S(2)}, u32[]{:S(2)}) collective-permute-start(f32[2,1024]{1,0:T(2,128)S(1)} %add.105), channel_id=1, source_target_pairs={{0,16},{1,17},{2,18},{3,19},{4,20},{5,21},{6,22},{7,23},{8,24},{9,... | collective-permute-start | bytes 24584 | tf_op jit(solution)/shard_map/ppermute | solution.py:166
  233.4 3.6 %fusion.39 = f32[896,1024]{1,0:T(8,128)S(1)} fusion(bf16[1024,896]{1,0:T(8,128)(2,1)} %collective-permute-done.11, bf16[1024,1024]{1,0:T(8,128)(2,1)S(1)} %bitcast.67), kind=kOutput, calls=%fused_computation.69 | convolution fusion | flops 1879048192 | bytes 7602176 | tf_op jit(solution)/shard_map/dot_general | solution.py:48
  237.2 3.5 %multiply_convert_fusion = bf16[896,1024]{1,0:T(8,128)(2,1)} fusion(f32[896,1024]{1,0:T(8,128)S(1)} %fusion.39, f32[1024]{0:T(1024)S(1)} %bitcast.78, bf16[1024,896]{1,0:T(8,128)(2,1)S(1)} %bitcast.70, bf16[1024,1024]{1,0:T(8,128)(2,1)S(1)} %bitcast.64), kind=kOutput, calls=%fused_computation | convolution fusion | flops 1883635712 | bytes 9441280 | tf_op jit(solution)/shard_map/dot_general | solution.py:48
  (82 shorter events, 52.1 us)
Async XLA Ops:
  0.6 98.7 %copy-start = (bf16[896,1024]{1,0:T(8,128)(2,1)S(1)}, bf16[896,1024]{1,0:T(8,128)(2,1)}, u32[]{:S(2)}) copy-start(bf16[896,1024]{1,0:T(8,128)(2,1)} %param.10) | copy-start | bytes 5505028
  0.6 77.9 %copy-start.7 = (bf16[128,896]{1,0:T(8,128)(2,1)S(1)}, bf16[128,896]{1,0:T(8,128)(2,1)}, u32[]{:S(2)}) copy-start(bf16[128,896]{1,0:T(8,128)(2,1)} %param.7) | copy-start | bytes 688132
  0.7 77.9 %copy-start.8 = (bf16[128,896]{1,0:T(8,128)(2,1)S(1)}, bf16[128,896]{1,0:T(8,128)(2,1)}, u32[]{:S(2)}) copy-start(bf16[128,896]{1,0:T(8,128)(2,1)} %param.8) | copy-start | bytes 688132
  40.7 17.9 %collective-permute-start = (bf16[8,64,1024]{2,1,0:T(8,128)(2,1)S(1)}, bf16[8,64,1024]{2,1,0:T(8,128)(2,1)S(1)}, u32[]{:S(2)}, u32[]{:S(2)}) collective-permute-start(bf16[8,64,1024]{2,1,0:T(8,128)(2,1)S(1)} %all_to_all.30.refs_0_), channel_id=1, source_target_pairs={{0,1},{1,2},{2,3},{3,0},{4,5},{5,6},{6,7},{7,4},{8,9},{9,10},{10,1... | collective-permute-start | bytes 3145736 | tf_op jit(solution)/shard_map/ppermute | solution.py:27
  58.6 18.0 %collective-permute-start.1 = (bf16[8,64,1024]{2,1,0:T(8,128)(2,1)S(1)}, bf16[8,64,1024]{2,1,0:T(8,128)(2,1)}, u32[]{:S(2)}, u32[]{:S(2)}) collective-permute-start(bf16[8,64,1024]{2,1,0:T(8,128)(2,1)S(1)} %collective-permute-done.refs_1_), channel_id=1, source_target_pairs={{0,1},{1,2},{2,3},{3,0},{4,5},{5,6},{6,7},{7,4},{8,9},{9,10},{10,1... | collective-permute-start | bytes 3145736 | tf_op jit(solution)/shard_map/ppermute | solution.py:27
  76.6 18.2 %collective-permute-start.2 = (bf16[8,64,1024]{2,1,0:T(8,128)(2,1)}, bf16[8,64,1024]{2,1,0:T(8,128)(2,1)}, u32[]{:S(2)}, u32[]{:S(2)}) collective-permute-start(bf16[8,64,1024]{2,1,0:T(8,128)(2,1)} %collective-permute-done.1.refs_2_), channel_id=1, source_target_pairs={{0,1},{1,2},{2,3},{3,0},{4,5},{5,6},{6,7},{7,4},{8,9},{9,10},{10,1... | collective-permute-start | bytes 3145736 | tf_op jit(solution)/shard_map/ppermute | solution.py:27
  78.7 69.2 %copy-start.4 = (bf16[128,896]{1,0:T(8,128)(2,1)}, bf16[128,896]{1,0:T(8,128)(2,1)S(1)}, u32[]{:S(2)}) copy-start(bf16[128,896]{1,0:T(8,128)(2,1)S(1)} %fusion.13.refs_0_) | copy-start | bytes 688132
  78.7 27.7 %collective-permute-start.4 = (bf16[128,896]{1,0:T(8,128)(2,1)S(1)}, bf16[128,896]{1,0:T(8,128)(2,1)}, u32[]{:S(2)}, u32[]{:S(2)}) collective-permute-start(bf16[128,896]{1,0:T(8,128)(2,1)S(1)} %fusion.13.refs_0_), channel_id=1, source_target_pairs={{0,256},{32,480},{256,64},{288,32},{64,320},{96,288},{320,128},{35... | collective-permute-start | bytes 688136 | tf_op jit(solution)/shard_map/ppermute | solution.py:34
  104.5 79.9 %collective-permute-start.3 = (bf16[1024,896]{1,0:T(8,128)(2,1)}, bf16[1024,896]{1,0:T(8,128)(2,1)}, u32[]{:S(2)}, u32[]{:S(2)}) collective-permute-start(bf16[1024,896]{1,0:T(8,128)(2,1)} %convolution_convert_fusion), channel_id=1, source_target_pairs={{0,32},{32,0},{64,96},{96,64},{128,160},{160,128},{192,224},{224,1... | collective-permute-start | bytes 5505032 | tf_op jit(solution)/shard_map/ppermute | solution.py:150
  106.4 8.1 %collective-permute-start.5 = (bf16[128,896]{1,0:T(8,128)(2,1)}, bf16[128,896]{1,0:T(8,128)(2,1)S(1)}, u32[]{:S(2)}, u32[]{:S(2)}) collective-permute-start(bf16[128,896]{1,0:T(8,128)(2,1)} %collective-permute-done.4.refs_1_), channel_id=1, source_target_pairs={{0,256},{32,480},{256,64},{288,32},{64,320},{96,288},{320,128},{35... | collective-permute-start | bytes 688136 | tf_op jit(solution)/shard_map/ppermute | solution.py:34
  114.6 29.2 %collective-permute-start.6 = (bf16[128,896]{1,0:T(8,128)(2,1)S(1)}, bf16[128,896]{1,0:T(8,128)(2,1)S(1)}, u32[]{:S(2)}, u32[]{:S(2)}) collective-permute-start(bf16[128,896]{1,0:T(8,128)(2,1)S(1)} %collective-permute-done.5.refs_2_), channel_id=1, source_target_pairs={{0,256},{32,480},{256,64},{288,32},{64,320},{96,288},{320,128},{35... | collective-permute-start | bytes 688136 | tf_op jit(solution)/shard_map/ppermute | solution.py:34
  143.8 9.2 %collective-permute-start.7 = (bf16[128,896]{1,0:T(8,128)(2,1)S(1)}, bf16[128,896]{1,0:T(8,128)(2,1)S(1)}, u32[]{:S(2)}, u32[]{:S(2)}) collective-permute-start(bf16[128,896]{1,0:T(8,128)(2,1)S(1)} %collective-permute-done.6.refs_3_), channel_id=1, source_target_pairs={{0,256},{32,480},{256,64},{288,32},{64,320},{96,288},{320,128},{35... | collective-permute-start | bytes 688136 | tf_op jit(solution)/shard_map/ppermute | solution.py:34
  149.1 15.2 %all-to-all-start.2 = ((bf16[32,16,128]{2,1,0:T(8,128)(2,1)}), bf16[32,16,128]{2,1,0:T(8,128)(2,1)S(1)}, u32[]{:S(2)}, u32[]{:S(2)}) async-start(bf16[32,16,128]{2,1,0:T(8,128)(2,1)} %bitcast.8), calls=%async_computation.2 | async-start | bytes 262144 | tf_op jit(solution)/shard_map/all_to_all | solution.py:141
  153.0 7.9 %collective-permute-start.8 = (bf16[128,896]{1,0:T(8,128)(2,1)S(1)}, bf16[128,896]{1,0:T(8,128)(2,1)S(1)}, u32[]{:S(2)}, u32[]{:S(2)}) collective-permute-start(bf16[128,896]{1,0:T(8,128)(2,1)S(1)} %collective-permute-done.7.refs_4_), channel_id=1, source_target_pairs={{0,256},{32,480},{256,64},{288,32},{64,320},{96,288},{320,128},{35... | collective-permute-start | bytes 688136 | tf_op jit(solution)/shard_map/ppermute | solution.py:34
  160.9 10.0 %collective-permute-start.9 = (bf16[128,896]{1,0:T(8,128)(2,1)S(1)}, bf16[128,896]{1,0:T(8,128)(2,1)}, u32[]{:S(2)}, u32[]{:S(2)}) collective-permute-start(bf16[128,896]{1,0:T(8,128)(2,1)S(1)} %collective-permute-done.8.refs_5_), channel_id=1, source_target_pairs={{0,256},{32,480},{256,64},{288,32},{64,320},{96,288},{320,128},{35... | collective-permute-start | bytes 688136 | tf_op jit(solution)/shard_map/ppermute | solution.py:34
  165.0 13.4 %all-to-all-start.3 = ((f32[16,16,128]{2,1,0:T(8,128)}), f32[16,16,128]{2,1,0:T(8,128)S(1)}, u32[]{:S(2)}, u32[]{:S(2)}) async-start(f32[16,16,128]{2,1,0:T(8,128)} %broadcast_in_dim.5), calls=%async_computation.3 | async-start | bytes 262144 | tf_op jit(solution)/shard_map/all_to_all | solution.py:144
  170.9 8.5 %collective-permute-start.10 = (bf16[128,896]{1,0:T(8,128)(2,1)}, bf16[128,896]{1,0:T(8,128)(2,1)}, u32[]{:S(2)}, u32[]{:S(2)}) collective-permute-start(bf16[128,896]{1,0:T(8,128)(2,1)} %collective-permute-done.9.refs_6_), channel_id=1, source_target_pairs={{0,256},{32,480},{256,64},{288,32},{64,320},{96,288},{320,128},{35... | collective-permute-start | bytes 688136 | tf_op jit(solution)/shard_map/ppermute | solution.py:34
  182.5 50.9 %collective-permute-start.11 = (bf16[1024,896]{1,0:T(8,128)(2,1)}, bf16[1024,896]{1,0:T(8,128)(2,1)}, u32[]{:S(2)}, u32[]{:S(2)}) collective-permute-start(bf16[1024,896]{1,0:T(8,128)(2,1)} %bitcast.69), channel_id=1, source_target_pairs={{0,32},{32,0},{64,96},{96,64},{128,160},{160,128},{192,224},{224,1... | collective-permute-start | bytes 5505032 | tf_op jit(solution)/shard_map/ppermute | solution.py:137
  190.2 52.7 %all-to-all-start.1 = ((bf16[8,128,896]{2,1,0:T(8,128)(2,1)}), bf16[8,128,896]{2,1,0:T(8,128)(2,1)}, u32[]{:S(2)}, u32[]{:S(2)}) async-start(bf16[8,128,896]{2,1,0:T(8,128)(2,1)} %bitcast.68), calls=%async_computation.1 | async-start | bytes 3670016 | tf_op jit(solution)/shard_map/all_to_all | solution.py:152
  201.9 5.5 %collective-permute-start.12 = (f32[2,1024]{1,0:T(2,128)S(1)}, f32[2,1024]{1,0:T(2,128)S(1)}, u32[]{:S(2)}, u32[]{:S(2)}) collective-permute-start(f32[2,1024]{1,0:T(2,128)S(1)} %pad_maximum_fusion), channel_id=1, source_target_pairs={{0,1},{1,0},{2,3},{3,2},{4,5},{5,4},{6,7},{7,6},{8,9},{9,8},{10,11... | collective-permute-start | bytes 24584 | tf_op jit(solution)/shard_map/ppermute | solution.py:166
  207.4 7.0 %collective-permute-start.13 = (f32[2,1024]{1,0:T(2,128)S(1)}, f32[2,1024]{1,0:T(2,128)S(1)}, u32[]{:S(2)}, u32[]{:S(2)}) collective-permute-start(f32[2,1024]{1,0:T(2,128)S(1)} %fusion.36), channel_id=1, source_target_pairs={{0,2},{1,3},{2,0},{3,1},{4,6},{5,7},{6,4},{7,5},{8,10},{9,11},{10,... | collective-permute-start | bytes 24584 | tf_op jit(solution)/shard_map/ppermute | solution.py:166
  214.5 5.5 %collective-permute-start.14 = (f32[2,1024]{1,0:T(2,128)S(1)}, f32[2,1024]{1,0:T(2,128)S(1)}, u32[]{:S(2)}, u32[]{:S(2)}) collective-permute-start(f32[2,1024]{1,0:T(2,128)S(1)} %fusion.52), channel_id=1, source_target_pairs={{0,4},{1,5},{2,6},{3,7},{4,0},{5,1},{6,2},{7,3},{8,12},{9,13},{10,... | collective-permute-start | bytes 24584 | tf_op jit(solution)/shard_map/ppermute | solution.py:166
  220.1 6.4 %collective-permute-start.15 = (f32[2,1024]{1,0:T(2,128)S(1)}, f32[2,1024]{1,0:T(2,128)S(1)}, u32[]{:S(2)}, u32[]{:S(2)}) collective-permute-start(f32[2,1024]{1,0:T(2,128)S(1)} %add.104), channel_id=1, source_target_pairs={{0,8},{1,9},{2,10},{3,11},{4,12},{5,13},{6,14},{7,15},{8,0},{9,1},... | collective-permute-start | bytes 24584 | tf_op jit(solution)/shard_map/ppermute | solution.py:166
  226.5 10.6 %collective-permute-start.16 = (f32[2,1024]{1,0:T(2,128)S(1)}, f32[2,1024]{1,0:T(2,128)S(1)}, u32[]{:S(2)}, u32[]{:S(2)}) collective-permute-start(f32[2,1024]{1,0:T(2,128)S(1)} %add.105), channel_id=1, source_target_pairs={{0,16},{1,17},{2,18},{3,19},{4,20},{5,21},{6,22},{7,23},{8,24},{9,... | collective-permute-start | bytes 24584 | tf_op jit(solution)/shard_map/ppermute | solution.py:166
  (13 other events, 269.4 us)
where the time goes:
time: 247 us; the launch traced here: 246 us
  starting transfers between devices  73.6 us (30%)
  waiting for transfers between devices  69.9 us (28%)
  blocking collectives  64.6 us (26%)
  matrix products  21.3 us (9%)
  Pallas kernels  7.56 us (3%)
  other arithmetic  5 us (2%)
  local copies, waits for them, and re-layouts  2.7 us (1%)
    ppermute x3, waiting for transfers between devices, along_x(): lax.ppermute(value, ('row', 'col'), [(source, 32 * row + c) for source, (...  42.3 us
    all_to_all x1, blocking collectives, gather_out(): lax.all_to_all(sent, 'col', 0, 0, tiled=True, axis_index_groups=Z_GROUPS)  38.8 us
    all_gather x1, blocking collectives, work(): basis_all = lax.all_gather(basis, TOK, axis=0, tiled=True)  25.7 us
    ppermute x7, starting transfers between devices, along_y(): lax.ppermute(value, TOK, [(index(y, q), index((y + 1 - 2 * q) % 8, q)) fo...  24.7 us
    ppermute x5, starting transfers between devices, work(): lax.ppermute(totals, 'col', [(c, c ^ bit) for c in range(32)])  19.8 us
    ppermute x5, waiting for transfers between devices, work(): lax.ppermute(totals, 'col', [(c, c ^ bit) for c in range(32)])  11.7 us
    dot_general x3, matrix products, dot_nt(): lax.dot_general(left, right, (((1,), (1,)), ((), ())), preferred_element_...  11.4 us
    ppermute x7, waiting for transfers between devices, along_y(): lax.ppermute(value, TOK, [(index(y, q), index((y + 1 - 2 * q) % 8, q)) fo...  10.2 us
  transfers between devices with their start and end apart: 20, of which 12 were waited for; matrix products, arithmetic and copies ran while one was open for 10% of the time, Pallas kernels for 3%

commit v1 on v0

v1 whole, which is shorter than its diff:
```python
import math

import jax
import jax.numpy as jnp
from jax import lax
from jax.experimental import pallas as pl
from jax.experimental.pallas import tpu as pltpu
from jax.sharding import PartitionSpec as P


first_fix = 1.0 - math.exp(1000.0 * math.log(0.9))
second_fix = 1.0 - math.exp(1000.0 * math.log(0.999))

BF = jnp.bfloat16
F32 = jnp.float32
TOK = ("dp", "row")
Z_GROUPS = [[4 * z + x for z in range(8)] for x in range(4)]
Y_GROUPS = [[2 * m + q for m in range(8)] for q in range(2)]
PAIR = [(k, k ^ 1) for k in range(16)]


def along_x(value):
    def target(row, c):
        return row, c - c % 4 + (c + 1 - 2 * (row % 2)) % 4

    moves = [(32 * row + c, target(row, c)) for row in range(8) for c in range(32)]
    return lax.ppermute(value, ("row", "col"), [(source, 32 * row + c) for source, (row, c) in moves])


def activation(gate_pre, up_pre):
    gate_f = gate_pre.astype(F32)
    sigma = jax.nn.sigmoid(gate_f)
    return gate_f, sigma, gate_f * sigma, up_pre.astype(F32)


def dot_nt(left, right):
    return lax.dot_general(left, right, (((1,), (1,)), ((), ())), preferred_element_type=F32)


def dot_tn(left, right):
    return lax.dot_general(left, right, (((0,), (0,)), ((), ())), preferred_element_type=F32)


def place_out_kernel(here_ref, *refs):
    pieces, out = refs[:-1], refs[-1]
    x, core = here_ref[0], here_ref[1]
    for step, piece in enumerate(pieces):
        out[:, lax.rem(x + 4 + step * (2 * core - 1), 4)] = piece[...]


def place_out(where, pieces):
    planes, rows, width = pieces[0].shape
    return pl.pallas_call(
        place_out_kernel,
        out_shape=jax.ShapeDtypeStruct((planes, 4, rows, width), BF),
        in_specs=[pl.BlockSpec(memory_space=pltpu.SMEM)] + [pl.BlockSpec(memory_space=pltpu.VMEM)] * 4,
        out_specs=pl.BlockSpec(memory_space=pltpu.VMEM),
        name="place_out",
    )(where, *pieces)


def gather_out(value):
    sent = jnp.broadcast_to(value[None], (8,) + value.shape).reshape((-1,) + value.shape[1:])
    got = lax.all_to_all(sent, "col", 0, 0, tiled=True, axis_index_groups=Z_GROUPS)
    pieces = [got.reshape((8,) + value.shape)]
    for _ in range(1, 4):
        pieces.append(along_x(pieces[-1]))
    return pieces


def exact(left, right):
    high = left.astype(BF)
    rest = left - high.astype(F32)
    mid = rest.astype(BF)
    low = (rest - mid.astype(F32)).astype(BF)
    terms = lax.dot_general(
        jnp.concatenate([high, mid, low], axis=0), right, (((1,), (0,)), ((), ())), preferred_element_type=F32
    ).reshape(3, 16, right.shape[1])
    return terms[0] + (terms[1] + terms[2])


def work(gate_pre, up_pre, grad_out, down_weight, basis, first_moment_in, second_moment_in):
    width = grad_out.shape[1]
    units = gate_pre.shape[1]
    core = lax.axis_index("row") % 2
    x = lax.axis_index("col") % 4
    pieces = gather_out(grad_out)

    _, _, act_early, up_early = activation(gate_pre, up_pre)
    hidden = (act_early * up_early).astype(BF)
    hidden_all = lax.all_gather(hidden, TOK, axis=0, tiled=True)

    basis_all = lax.all_gather(basis, TOK, axis=0, tiled=True)
    tp_part = dot_nt(basis_all, hidden).astype(BF)
    tp_got = lax.all_to_all(tp_part, "col", 0, 0, tiled=True).reshape(32, 16, 128)
    tp_mine = jnp.sum(tp_got.astype(F32), axis=0)
    tp_sent = jnp.broadcast_to(tp_mine[None], (16, 16, 128)).reshape(256, 128)
    tp_all = lax.all_to_all(tp_sent, TOK, 0, 0, tiled=True).reshape(16, 16, 128).transpose(1, 0, 2).reshape(16, 2048)

    parts = []
    for piece in pieces:
        parts.append(dot_nt(piece.reshape(512, width), down_weight).astype(BF))
    sums = []
    for first, second, source in ((0, 2, x), (1, 3, (x + 3 + 2 * core) % 4)):
        first_mine = source // 2 == core
        other = jnp.where(first_mine, parts[second], parts[first])
        mine = jnp.where(first_mine, parts[first], parts[second])
        got = lax.ppermute(other, TOK, PAIR)
        sums.append((mine.astype(F32) + got.astype(F32)).astype(BF).reshape(8, 64, units))
    part_sum = jnp.stack(sums, axis=1).reshape(1024, units)
    blocks = lax.all_to_all(part_sum, TOK, 0, 0, tiled=True, axis_index_groups=Y_GROUPS)
    summed = jnp.sum(blocks.reshape(8, 2, 64, units).astype(F32), axis=0).astype(BF)
    summed = jnp.where(x % 2 == 0, summed, summed[::-1]).reshape(128, units)
    gate_late, up_late, summed = lax.optimization_barrier((gate_pre, up_pre, summed))
    gate_f, sigma, act_value, up_f = activation(gate_late, up_late)
    grad_hidden = summed.astype(F32)
    grad_up = (grad_hidden * act_value).astype(BF)
    grad_gate = (grad_hidden * up_f * sigma * (1.0 + gate_f * (1.0 - sigma))).astype(BF)

    out_all = place_out(jnp.stack([x, core]), pieces).reshape(2048, width)
    projected = exact(tp_all, out_all)
    first_moment = 0.9 * first_moment_in + 0.1 * projected
    second_moment = 0.999 * second_moment_in + 0.001 * projected * projected
    adapted = first_moment / first_fix / (jnp.sqrt(second_moment / second_fix) + 1e-06)
    totals = jnp.stack([jnp.sum(adapted * adapted, axis=0), jnp.sum(projected * projected, axis=0)])
    for bit in (1, 2, 4, 8, 16):
        totals = totals + lax.ppermute(totals, "col", [(c, c ^ bit) for c in range(32)])
    column_scale = jnp.sqrt(totals[0]) / (jnp.sqrt(totals[1]) + 1e-06)

    grad_weight = dot_tn(hidden_all, out_all).astype(BF)
    scaled_grad = (grad_weight.astype(F32) * column_scale[None, :]).astype(BF)
    return (grad_gate, grad_up, scaled_grad, first_moment, second_moment)


def solution(mesh):
    rows = P(TOK, "col")
    cols = P("col", TOK)
    return jax.shard_map(
        work,
        mesh=mesh,
        in_specs=(rows, rows, cols, cols, rows, cols, cols),
        out_specs=(rows, rows, cols, cols, cols),
        check_vma=False,
    )
```

time: 247 us -> 221 us (0.89)
  starting transfers between devices: 73.6 us -> 46.8 us
  waiting for transfers between devices: 69.9 us -> 49.9 us
  between operations: 1.16 us -> 14.5 us
  blocking collectives: 64.6 us -> 69.8 us
  other arithmetic: 5 us -> 9.97 us
  Pallas kernels: 7.56 us -> 4.39 us
    ppermute x3, waiting for transfers between devices: 42.3 us -> 16.7 us  [along_x(): lax.ppermute(value, ('row', 'col'), [(source, 32 * row + c) for source, (...]
    ppermute x9 -> x2, starting transfers between devices: 28.5 us -> 5 us  [work(): got = lax.ppermute(other, TOK, PAIR)]
    all_to_all x1, waiting for transfers between devices: 0.01 us -> 10.5 us  [work(): lax.all_to_all(tp_part, 'col', 0, 0, tiled=True).reshape(32, 16, 128)]
    ppermute x9 -> x2, waiting for transfers between devices: 10.2 us -> 0.01 us  [work(): got = lax.ppermute(other, TOK, PAIR)]
    ppermute x5, waiting for transfers between devices: 11.7 us -> 20.1 us  [work(): lax.ppermute(totals, 'col', [(c, c ^ bit) for c in range(32)])]
    ppermute x5, starting transfers between devices: 19.8 us -> 13.9 us  [work(): lax.ppermute(totals, 'col', [(c, c ^ bit) for c in range(32)])]
    all_gather x1, blocking collectives: 25.7 us -> 30.8 us  [work(): basis_all = lax.all_gather(basis, TOK, axis=0, tiled=True)]
    convert_element_type x0 -> x2, other arithmetic: none -> 3.41 us  [work(): (mine.astype(F32) + got.astype(F32)).astype(BF).reshape(8, 64, units)]
  transfers between devices with their start and end apart: 20 -> 14, of which waited for: 12 -> 9; matrix products, arithmetic and copies ran while one was open for 10% -> 14% of each run, Pallas kernels for 3% -> 2%
where the time goes in v1:
time: 221 us; the launch traced here: 220 us
  blocking collectives  69.8 us (32%)
  waiting for transfers between devices  49.9 us (23%)
  starting transfers between devices  46.8 us (21%)
  matrix products  22.5 us (10%)
  between operations  14.5 us (7%)
  other arithmetic  9.97 us (5%)
  Pallas kernels  4.39 us (2%)
  local copies, waits for them, and re-layouts  2.65 us (1%)
    all_to_all x1, blocking collectives, gather_out(): lax.all_to_all(sent, 'col', 0, 0, tiled=True, axis_index_groups=Z_GROUPS)  39 us
    all_gather x1, blocking collectives, work(): basis_all = lax.all_gather(basis, TOK, axis=0, tiled=True)  30.8 us
    ppermute x5, waiting for transfers between devices, work(): lax.ppermute(totals, 'col', [(c, c ^ bit) for c in range(32)])  20.1 us
    ppermute x3, waiting for transfers between devices, along_x(): lax.ppermute(value, ('row', 'col'), [(source, 32 * row + c) for source, (...  16.7 us
    ppermute x5, starting transfers between devices, work(): lax.ppermute(totals, 'col', [(c, c ^ bit) for c in range(32)])  13.9 us
    dot_general x5, matrix products, dot_nt(): lax.dot_general(left, right, (((1,), (1,)), ((), ())), preferred_element_...  10.9 us
    all_to_all x1, waiting for transfers between devices, work(): lax.all_to_all(tp_part, 'col', 0, 0, tiled=True).reshape(32, 16, 128)  10.5 us
    ppermute x3, starting transfers between devices, along_x(): lax.ppermute(value, ('row', 'col'), [(source, 32 * row + c) for source, (...  10.2 us
  transfers between devices with their start and end apart: 14, of which 9 were waited for; matrix products, arithmetic and copies ran while one was open for 14% of the time, Pallas kernels for 2%

profile of v1, /device:TPU:8, one launch (start us, length us, event | category | flops | bytes accessed | tf_op | source)
XLA Modules:
  0.0 220.5 jit_solution(6220100906784208869)
XLA Ops:
  8.4 39.0 %all_to_all.33.refs_0_ = bf16[8,64,1024]{2,1,0:T(8,128)(2,1)S(1)} all-to-all(bf16[8,64,1024]{2,1,0:T(8,128)(2,1)S(1)} %broadcast_in_dim.4), channel_id=1, replica_groups={{0,4,8,12,16,20,24,28},{1,5,9,13,17,21,25,29},{2,6,10,14,18,22,26,30},{..., dimensions={0} | all-to-all | bytes 2097152 | tf_op jit(solution)/shard_map/all_to_all | solution.py:64
  47.4 3.4 %collective-permute-start = (bf16[8,64,1024]{2,1,0:T(8,128)(2,1)S(1)}, bf16[8,64,1024]{2,1,0:T(8,128)(2,1)}, u32[]{:S(2)}, u32[]{:S(2)}) collective-permute-start(bf16[8,64,1024]{2,1,0:T(8,128)(2,1)S(1)} %all_to_all.33.refs_0_), channel_id=1, source_target_pairs={{0,1},{1,2},{2,3},{3,0},{4,5},{5,6},{6,7},{7,4},{8,9},{9,10},{10,1... | collective-permute-start | bytes 3145736 | tf_op jit(solution)/shard_map/ppermute | solution.py:27
  51.7 13.7 %collective-permute-done.refs_1_ = bf16[8,64,1024]{2,1,0:T(8,128)(2,1)} collective-permute-done((bf16[8,64,1024]{2,1,0:T(8,128)(2,1)S(1)}, bf16[8,64,1024]{2,1,0:T(8,128)(2,1)}, u32[]{:S(2)}, u32[]{:S(2)}) %collective-permute-start) | collective-permute-done | bytes 1048608 | tf_op jit(solution)/shard_map/ppermute | solution.py:27
  67.7 30.8 %all_gather.7 = bf16[512,896]{1,0:T(8,128)(2,1)S(1)} all-gather(bf16[32,896]{1,0:T(8,128)(2,1)S(1)} %copy-done.10), channel_id=1, replica_groups=mesh['dp'=2,'row'=8,'col'=32] {'dp','row'}, dimensions={0}, use_global_device_ids=true | all-gather | bytes 974848 | tf_op jit(solution)/shard_map/all_gather | solution.py:93
  98.5 4.7 %collective-permute-start.3 = (bf16[8,64,1024]{2,1,0:T(8,128)(2,1)}, bf16[8,64,1024]{2,1,0:T(8,128)(2,1)S(1)}, u32[]{:S(2)}, u32[]{:S(2)}) collective-permute-start(bf16[8,64,1024]{2,1,0:T(8,128)(2,1)} %collective-permute-done.1.refs_2_), channel_id=1, source_target_pairs={{0,1},{1,2},{2,3},{3,0},{4,5},{5,6},{6,7},{7,4},{8,9},{9,10},{10,1... | collective-permute-start | bytes 3145736 | tf_op jit(solution)/shard_map/ppermute | solution.py:27
  104.5 2.8 %convolution_convert_fusion.1 = bf16[512,896]{1,0:T(8,128)(2,1)S(1)} fusion(bf16[512,1024]{1,0:T(8,128)(2,1)} %bitcast.4, bf16[896,1024]{1,0:T(8,128)(2,1)S(1)} %copy-done), kind=kOutput, calls=%fused_computation.5 | convolution fusion | flops 939982848 | bytes 3801088 | tf_op jit(solution)/shard_map/dot_general | solution.py:37
  107.3 3.8 %broadcast_select_fusion.1 = (bf16[512,896]{1,0:T(8,128)(2,1)}, bf16[512,896]{1,0:T(8,128)(2,1)}) fusion(bf16[512,896]{1,0:T(8,128)(2,1)S(1)} %convolution_convert_fusion.3, pred[]{:T(512)S(6)} %eq.15, bf16[512,1024]{1,0:T(8,128)(2,1)} %bitcast.1, bf16[896,1024]{1,0:T(8,128)(2,1)S(1)} %copy-done), kind=kOutput, calls=%fused_computation.11 | convolution fusion | flops 940441600 | bytes 5636097 | tf_op jit(solution)/shard_map/dot_general | solution.py:37
  111.1 3.1 %collective-permute-start.2 = (bf16[512,896]{1,0:T(8,128)(2,1)}, bf16[512,896]{1,0:T(8,128)(2,1)}, u32[]{:S(2)}, u32[]{:S(2)}) collective-permute-start(bf16[512,896]{1,0:T(8,128)(2,1)} %get-tuple-element.21), channel_id=1, source_target_pairs={{0,32},{32,0},{64,96},{96,64},{128,160},{160,128},{192,224},{224,1... | collective-permute-start | bytes 2752520 | tf_op jit(solution)/shard_map/ppermute | solution.py:108
  114.2 3.0 %collective-permute-done.3.refs_3_ = bf16[8,64,1024]{2,1,0:T(8,128)(2,1)S(1)} collective-permute-done((bf16[8,64,1024]{2,1,0:T(8,128)(2,1)}, bf16[8,64,1024]{2,1,0:T(8,128)(2,1)S(1)}, u32[]{:S(2)}, u32[]{:S(2)}) %collective-permute-start.3) | collective-permute-done | bytes 1048608 | tf_op jit(solution)/shard_map/ppermute | solution.py:27
  122.9 5.1 %all-to-all-start.2 = ((bf16[32,16,128]{2,1,0:T(8,128)(2,1)}), bf16[32,16,128]{2,1,0:T(8,128)(2,1)S(1)}, u32[]{:S(2)}, u32[]{:S(2)}) async-start(bf16[32,16,128]{2,1,0:T(8,128)(2,1)} %bitcast.15), calls=%async_computation.2 | async-start | bytes 262144 | tf_op jit(solution)/shard_map/all_to_all | solution.py:95
  128.6 10.5 %all-to-all-done.2 = bf16[32,16,128]{2,1,0:T(8,128)(2,1)S(1)} async-done(((bf16[32,16,128]{2,1,0:T(8,128)(2,1)}), bf16[32,16,128]{2,1,0:T(8,128)(2,1)S(1)}, u32[]{:S(2)}, u32[]{:S(2)}) %all-to-all-start.2) | async-done | bytes 131104 | tf_op jit(solution)/shard_map/all_to_all | solution.py:95
  139.8 6.7 %all-to-all-start.3 = ((f32[16,16,128]{2,1,0:T(8,128)}), f32[16,16,128]{2,1,0:T(8,128)S(1)}, u32[]{:S(2)}, u32[]{:S(2)}) async-start(f32[16,16,128]{2,1,0:T(8,128)} %broadcast_in_dim.5), calls=%async_computation.3 | async-start | bytes 262144 | tf_op jit(solution)/shard_map/all_to_all | solution.py:98
  154.1 5.8 %all-to-all-start.1 = ((bf16[8,128,896]{2,1,0:T(8,128)(2,1)}), bf16[8,128,896]{2,1,0:T(8,128)(2,1)}, u32[]{:S(2)}, u32[]{:S(2)}) async-start(bf16[8,128,896]{2,1,0:T(8,128)(2,1)} %bitcast.56), calls=%async_computation.1 | async-start | bytes 3670016 | tf_op jit(solution)/shard_map/all_to_all | solution.py:111
  159.9 4.4 %place_out.1 = bf16[8,4,64,1024]{3,2,1,0:T(8,128)(2,1)} custom-call(s32[2]{0:T(128)} %pad_add_fusion.here_ref, bf16[8,64,1024]{2,1,0:T(8,128)(2,1)} %copy-done.1, bf16[8,64,1024]{2,1,0:T(8,128)(2,1)} %collective-permute-done.refs_1_, bf16[8,64,1024]{2,1,0:T(8,128)(2,1)} %collective-permute-done.1.refs_2_, bf16[8,64,1024]{2,1,0:T(8,128)(2,1)} %copy-done.3), custom_call_target="tpu_custom_call" | custom-call | tf_op jit(solution)/shard_map/place_out/pallas_call | solution.py:53
  164.3 3.1 %fusion.14 = f32[48,1024]{1,0:T(8,128)S(1)} fusion(bf16[2048,1024]{1,0:T(8,128)(2,1)} %bitcast.54, bf16[16,2048]{1,0:T(8,128)(2,1)S(1)} %get-tuple-element.18, bf16[16,2048]{1,0:T(8,128)(2,1)S(1)} %get-tuple-element.17, bf16[16,2048]{1,0:T(8,128)(2,1)S(1)} %bitcast_convert_fusion), kind=kOutput, calls=%fused_computation.34 | convolution fusion | flops 201916416 | bytes 4587520 | tf_op jit(solution)/shard_map/dot_general | solution.py:76
  170.1 3.6 %collective-permute-done.5 = f32[2,1024]{1,0:T(2,128)S(1)} collective-permute-done((f32[2,1024]{1,0:T(2,128)S(1)}, f32[2,1024]{1,0:T(2,128)S(1)}, u32[]{:S(2)}, u32[]{:S(2)}) %collective-permute-start.5) | collective-permute-done | bytes 8224 | tf_op jit(solution)/shard_map/ppermute | solution.py:127
  173.6 3.1 %collective-permute-start.6 = (f32[2,1024]{1,0:T(2,128)S(1)}, f32[2,1024]{1,0:T(2,128)S(1)}, u32[]{:S(2)}, u32[]{:S(2)}) collective-permute-start(f32[2,1024]{1,0:T(2,128)S(1)} %fusion.26), channel_id=1, source_target_pairs={{0,2},{1,3},{2,0},{3,1},{4,6},{5,7},{6,4},{7,5},{8,10},{9,11},{10,... | collective-permute-start | bytes 24584 | tf_op jit(solution)/shard_map/ppermute | solution.py:127
  176.8 3.9 %collective-permute-done.6 = f32[2,1024]{1,0:T(2,128)S(1)} collective-permute-done((f32[2,1024]{1,0:T(2,128)S(1)}, f32[2,1024]{1,0:T(2,128)S(1)}, u32[]{:S(2)}, u32[]{:S(2)}) %collective-permute-start.6) | collective-permute-done | bytes 8224 | tf_op jit(solution)/shard_map/ppermute | solution.py:127
  180.7 2.8 %collective-permute-start.7 = (f32[2,1024]{1,0:T(2,128)S(1)}, f32[2,1024]{1,0:T(2,128)S(1)}, u32[]{:S(2)}, u32[]{:S(2)}) collective-permute-start(f32[2,1024]{1,0:T(2,128)S(1)} %fusion.42), channel_id=1, source_target_pairs={{0,4},{1,5},{2,6},{3,7},{4,0},{5,1},{6,2},{7,3},{8,12},{9,13},{10,... | collective-permute-start | bytes 24584 | tf_op jit(solution)/shard_map/ppermute | solution.py:127
  186.3 2.8 %collective-permute-start.8 = (f32[2,1024]{1,0:T(2,128)S(1)}, f32[2,1024]{1,0:T(2,128)S(1)}, u32[]{:S(2)}, u32[]{:S(2)}) collective-permute-start(f32[2,1024]{1,0:T(2,128)S(1)} %add.95), channel_id=1, source_target_pairs={{0,8},{1,9},{2,10},{3,11},{4,12},{5,13},{6,14},{7,15},{8,0},{9,1},... | collective-permute-start | bytes 24584 | tf_op jit(solution)/shard_map/ppermute | solution.py:127
  189.1 3.6 %collective-permute-done.8 = f32[2,1024]{1,0:T(2,128)S(1)} collective-permute-done((f32[2,1024]{1,0:T(2,128)S(1)}, f32[2,1024]{1,0:T(2,128)S(1)}, u32[]{:S(2)}, u32[]{:S(2)}) %collective-permute-start.8) | collective-permute-done | bytes 8224 | tf_op jit(solution)/shard_map/ppermute | solution.py:127
  192.7 3.1 %collective-permute-start.9 = (f32[2,1024]{1,0:T(2,128)S(1)}, f32[2,1024]{1,0:T(2,128)S(1)}, u32[]{:S(2)}, u32[]{:S(2)}) collective-permute-start(f32[2,1024]{1,0:T(2,128)S(1)} %add.96), channel_id=1, source_target_pairs={{0,16},{1,17},{2,18},{3,19},{4,20},{5,21},{6,22},{7,23},{8,24},{9,... | collective-permute-start | bytes 24584 | tf_op jit(solution)/shard_map/ppermute | solution.py:127
  195.9 6.3 %collective-permute-done.9 = f32[2,1024]{1,0:T(2,128)S(1)} collective-permute-done((f32[2,1024]{1,0:T(2,128)S(1)}, f32[2,1024]{1,0:T(2,128)S(1)}, u32[]{:S(2)}, u32[]{:S(2)}) %collective-permute-start.9) | collective-permute-done | bytes 8224 | tf_op jit(solution)/shard_map/ppermute | solution.py:127
  202.2 8.5 %multiply_convert_fusion = bf16[896,1024]{1,0:T(8,128)(2,1)} fusion(f32[1024]{0:T(1024)S(1)} %bitcast.69, bf16[2048,896]{1,0:T(8,128)(2,1)} %all-gather.2.cloned.1.call-done, bf16[2048,1024]{1,0:T(8,128)(2,1)} %bitcast.55), kind=kOutput, calls=%fused_computation | convolution fusion | flops 3761766400 | bytes 9703424 | tf_op jit(solution)/shard_map/dot_general | solution.py:41
  (60 shorter events, 28.4 us)
Async XLA Ops:
  7.2 96.0 %copy-start = (bf16[896,1024]{1,0:T(8,128)(2,1)S(1)}, bf16[896,1024]{1,0:T(8,128)(2,1)}, u32[]{:S(2)}) copy-start(bf16[896,1024]{1,0:T(8,128)(2,1)} %param.10) | copy-start | bytes 5505028
  7.2 43.6 %copy-start.6 = (bf16[128,896]{1,0:T(8,128)(2,1)S(1)}, bf16[128,896]{1,0:T(8,128)(2,1)}, u32[]{:S(2)}) copy-start(bf16[128,896]{1,0:T(8,128)(2,1)} %param.7) | copy-start | bytes 688132
  7.2 43.6 %copy-start.7 = (bf16[128,896]{1,0:T(8,128)(2,1)S(1)}, bf16[128,896]{1,0:T(8,128)(2,1)}, u32[]{:S(2)}) copy-start(bf16[128,896]{1,0:T(8,128)(2,1)} %param.8) | copy-start | bytes 688132
  7.2 195.0 %all-gather.2.cloned.1.call-start = ((), (), s32[]{:S(2)}) async-start(), calls=%async_computation.4 | async-start | bytes 3899392 | tf_op jit(solution)/shard_map/all_gather | solution.py:91
  8.4 59.3 %copy-start.10 = (bf16[32,896]{1,0:T(8,128)(2,1)S(1)}, bf16[32,896]{1,0:T(8,128)(2,1)}, u32[]{:S(2)}) copy-start(bf16[32,896]{1,0:T(8,128)(2,1)} %param.11) | copy-start | bytes 172036
  47.4 57.0 %copy-start.1 = (bf16[8,64,1024]{2,1,0:T(8,128)(2,1)}, bf16[8,64,1024]{2,1,0:T(8,128)(2,1)S(1)}, u32[]{:S(2)}) copy-start(bf16[8,64,1024]{2,1,0:T(8,128)(2,1)S(1)} %all_to_all.33.refs_0_) | copy-start | bytes 3145732
  47.4 18.0 %collective-permute-start = (bf16[8,64,1024]{2,1,0:T(8,128)(2,1)S(1)}, bf16[8,64,1024]{2,1,0:T(8,128)(2,1)}, u32[]{:S(2)}, u32[]{:S(2)}) collective-permute-start(bf16[8,64,1024]{2,1,0:T(8,128)(2,1)S(1)} %all_to_all.33.refs_0_), channel_id=1, source_target_pairs={{0,1},{1,2},{2,3},{3,0},{4,5},{5,6},{6,7},{7,4},{8,9},{9,10},{10,1... | collective-permute-start | bytes 3145736 | tf_op jit(solution)/shard_map/ppermute | solution.py:27
  65.4 33.1 %collective-permute-start.1 = (bf16[8,64,1024]{2,1,0:T(8,128)(2,1)}, bf16[8,64,1024]{2,1,0:T(8,128)(2,1)}, u32[]{:S(2)}, u32[]{:S(2)}) collective-permute-start(bf16[8,64,1024]{2,1,0:T(8,128)(2,1)} %collective-permute-done.refs_1_), channel_id=1, source_target_pairs={{0,1},{1,2},{2,3},{3,0},{4,5},{5,6},{6,7},{7,4},{8,9},{9,10},{10,1... | collective-permute-start | bytes 3145736 | tf_op jit(solution)/shard_map/ppermute | solution.py:27
  98.5 18.8 %collective-permute-start.3 = (bf16[8,64,1024]{2,1,0:T(8,128)(2,1)}, bf16[8,64,1024]{2,1,0:T(8,128)(2,1)S(1)}, u32[]{:S(2)}, u32[]{:S(2)}) collective-permute-start(bf16[8,64,1024]{2,1,0:T(8,128)(2,1)} %collective-permute-done.1.refs_2_), channel_id=1, source_target_pairs={{0,1},{1,2},{2,3},{3,0},{4,5},{5,6},{6,7},{7,4},{8,9},{9,10},{10,1... | collective-permute-start | bytes 3145736 | tf_op jit(solution)/shard_map/ppermute | solution.py:27
  104.5 2.9 %copy-start.4 = (bf16[512,896]{1,0:T(8,128)(2,1)}, bf16[512,896]{1,0:T(8,128)(2,1)S(1)}, u32[]{:S(2)}) copy-start(bf16[512,896]{1,0:T(8,128)(2,1)S(1)} %convolution_convert_fusion.3) | copy-start | bytes 2752516
  111.1 35.5 %collective-permute-start.2 = (bf16[512,896]{1,0:T(8,128)(2,1)}, bf16[512,896]{1,0:T(8,128)(2,1)}, u32[]{:S(2)}, u32[]{:S(2)}) collective-permute-start(bf16[512,896]{1,0:T(8,128)(2,1)} %get-tuple-element.21), channel_id=1, source_target_pairs={{0,32},{32,0},{64,96},{96,64},{128,160},{160,128},{192,224},{224,1... | collective-permute-start | bytes 2752520 | tf_op jit(solution)/shard_map/ppermute | solution.py:108
  117.2 2.6 %copy-start.3 = (bf16[8,64,1024]{2,1,0:T(8,128)(2,1)}, bf16[8,64,1024]{2,1,0:T(8,128)(2,1)S(1)}, u32[]{:S(2)}) copy-start(bf16[8,64,1024]{2,1,0:T(8,128)(2,1)S(1)} %collective-permute-done.3.refs_3_) | copy-start | bytes 3145732
  117.2 4.5 %copy-start.2 = (bf16[128,896]{1,0:T(8,128)(2,1)S(1)}, bf16[128,896]{1,0:T(8,128)(2,1)}, u32[]{:S(2)}) copy-start(bf16[128,896]{1,0:T(8,128)(2,1)} %fusion.13) | copy-start | bytes 688132
  119.8 28.7 %collective-permute-start.4 = (bf16[512,896]{1,0:T(8,128)(2,1)}, bf16[512,896]{1,0:T(8,128)(2,1)}, u32[]{:S(2)}, u32[]{:S(2)}) collective-permute-start(bf16[512,896]{1,0:T(8,128)(2,1)} %get-tuple-element.19), channel_id=1, source_target_pairs={{0,32},{32,0},{64,96},{96,64},{128,160},{160,128},{192,224},{224,1... | collective-permute-start | bytes 2752520 | tf_op jit(solution)/shard_map/ppermute | solution.py:108
  122.9 16.2 %all-to-all-start.2 = ((bf16[32,16,128]{2,1,0:T(8,128)(2,1)}), bf16[32,16,128]{2,1,0:T(8,128)(2,1)S(1)}, u32[]{:S(2)}, u32[]{:S(2)}) async-start(bf16[32,16,128]{2,1,0:T(8,128)(2,1)} %bitcast.15), calls=%async_computation.2 | async-start | bytes 262144 | tf_op jit(solution)/shard_map/all_to_all | solution.py:95
  139.8 14.2 %all-to-all-start.3 = ((f32[16,16,128]{2,1,0:T(8,128)}), f32[16,16,128]{2,1,0:T(8,128)S(1)}, u32[]{:S(2)}, u32[]{:S(2)}) async-start(f32[16,16,128]{2,1,0:T(8,128)} %broadcast_in_dim.5), calls=%async_computation.3 | async-start | bytes 262144 | tf_op jit(solution)/shard_map/all_to_all | solution.py:98
  154.1 56.7 %all-to-all-start.1 = ((bf16[8,128,896]{2,1,0:T(8,128)(2,1)}), bf16[8,128,896]{2,1,0:T(8,128)(2,1)}, u32[]{:S(2)}, u32[]{:S(2)}) async-start(bf16[8,128,896]{2,1,0:T(8,128)(2,1)} %bitcast.56), calls=%async_computation.1 | async-start | bytes 3670016 | tf_op jit(solution)/shard_map/all_to_all | solution.py:111
  164.3 3.1 %copy-start.8 = (f32[16,1024]{1,0:T(8,128)S(1)}, f32[16,1024]{1,0:T(8,128)}, u32[]{:S(2)}) copy-start(f32[16,1024]{1,0:T(8,128)} %param.13) | copy-start | bytes 196612
  164.3 3.1 %copy-start.9 = (f32[16,1024]{1,0:T(8,128)S(1)}, f32[16,1024]{1,0:T(8,128)}, u32[]{:S(2)}) copy-start(f32[16,1024]{1,0:T(8,128)} %param.12) | copy-start | bytes 196612
  168.1 5.5 %collective-permute-start.5 = (f32[2,1024]{1,0:T(2,128)S(1)}, f32[2,1024]{1,0:T(2,128)S(1)}, u32[]{:S(2)}, u32[]{:S(2)}) collective-permute-start(f32[2,1024]{1,0:T(2,128)S(1)} %pad_maximum_fusion.1), channel_id=1, source_target_pairs={{0,1},{1,0},{2,3},{3,2},{4,5},{5,4},{6,7},{7,6},{8,9},{9,8},{10,11... | collective-permute-start | bytes 24584 | tf_op jit(solution)/shard_map/ppermute | solution.py:127
  173.6 7.0 %collective-permute-start.6 = (f32[2,1024]{1,0:T(2,128)S(1)}, f32[2,1024]{1,0:T(2,128)S(1)}, u32[]{:S(2)}, u32[]{:S(2)}) collective-permute-start(f32[2,1024]{1,0:T(2,128)S(1)} %fusion.26), channel_id=1, source_target_pairs={{0,2},{1,3},{2,0},{3,1},{4,6},{5,7},{6,4},{7,5},{8,10},{9,11},{10,... | collective-permute-start | bytes 24584 | tf_op jit(solution)/shard_map/ppermute | solution.py:127
  180.7 5.5 %collective-permute-start.7 = (f32[2,1024]{1,0:T(2,128)S(1)}, f32[2,1024]{1,0:T(2,128)S(1)}, u32[]{:S(2)}, u32[]{:S(2)}) collective-permute-start(f32[2,1024]{1,0:T(2,128)S(1)} %fusion.42), channel_id=1, source_target_pairs={{0,4},{1,5},{2,6},{3,7},{4,0},{5,1},{6,2},{7,3},{8,12},{9,13},{10,... | collective-permute-start | bytes 24584 | tf_op jit(solution)/shard_map/ppermute | solution.py:127
  186.3 6.4 %collective-permute-start.8 = (f32[2,1024]{1,0:T(2,128)S(1)}, f32[2,1024]{1,0:T(2,128)S(1)}, u32[]{:S(2)}, u32[]{:S(2)}) collective-permute-start(f32[2,1024]{1,0:T(2,128)S(1)} %add.95), channel_id=1, source_target_pairs={{0,8},{1,9},{2,10},{3,11},{4,12},{5,13},{6,14},{7,15},{8,0},{9,1},... | collective-permute-start | bytes 24584 | tf_op jit(solution)/shard_map/ppermute | solution.py:127
  192.7 9.4 %collective-permute-start.9 = (f32[2,1024]{1,0:T(2,128)S(1)}, f32[2,1024]{1,0:T(2,128)S(1)}, u32[]{:S(2)}, u32[]{:S(2)}) collective-permute-start(f32[2,1024]{1,0:T(2,128)S(1)} %add.96), channel_id=1, source_target_pairs={{0,16},{1,17},{2,18},{3,19},{4,20},{5,21},{6,22},{7,23},{8,24},{9,... | collective-permute-start | bytes 24584 | tf_op jit(solution)/shard_map/ppermute | solution.py:127
  (1 other events, 1.9 us)
Sparse Core Ops, SparseCore 0:
  51.8 76.8 all-gather.1

commit v2 on v0

--- a/solution.py
+++ b/solution.py
@@ -94,13 +94,13 @@
     )(where, *pieces)
 
 
-def gather_out(value, where):
+def gather_out(value):
     sent = jnp.broadcast_to(value[None], (8,) + value.shape).reshape((-1,) + value.shape[1:])
     got = lax.all_to_all(sent, "col", 0, 0, tiled=True, axis_index_groups=Z_GROUPS)
     pieces = [got.reshape((8,) + value.shape)]
     for _ in range(1, 4):
         pieces.append(along_x(pieces[-1]))
-    return place_out(where, pieces)
+    return pieces
 
 
 def gather_hid(value, where):
@@ -127,9 +127,7 @@
     core = lax.axis_index("row") % 2
     y = 2 * (lax.axis_index("row") // 2) + lax.axis_index("dp")
     x = lax.axis_index("col") % 4
-
-    out_own, out_other = gather_out(grad_out, jnp.stack([x, core]))
-    out_own, out_other = out_own.reshape(1024, width), out_other.reshape(1024, width)
+    pieces = gather_out(grad_out)
 
     _, _, act_early, up_early = activation(gate_pre, up_pre)
     hidden = (act_early * up_early).astype(BF)
@@ -146,17 +144,28 @@
     def tp_rows(which):
         return lax.dynamic_index_in_dim(tp_all, which, 1, keepdims=False).transpose(1, 0, 2).reshape(16, 1024)
 
-    part_other = dot_nt(out_other, down_weight).astype(BF)
-    part_got = lax.ppermute(part_other, TOK, PAIR)
-    part_sum = (dot_nt(out_own, down_weight) + part_got.astype(F32)).astype(BF)
+    parts = []
+    for piece in pieces:
+        parts.append(dot_nt(piece.reshape(512, width), down_weight).astype(BF))
+    sums = []
+    for first, second, source in ((0, 2, x), (1, 3, (x + 3 + 2 * core) % 4)):
+        first_mine = source // 2 == core
+        other = jnp.where(first_mine, parts[second], parts[first])
+        mine = jnp.where(first_mine, parts[first], parts[second])
+        got = lax.ppermute(other, TOK, PAIR)
+        sums.append((mine.astype(F32) + got.astype(F32)).astype(BF).reshape(8, 64, units))
+    part_sum = jnp.stack(sums, axis=1).reshape(1024, units)
     blocks = lax.all_to_all(part_sum, TOK, 0, 0, tiled=True, axis_index_groups=Y_GROUPS)
-    summed = jnp.sum(blocks.reshape(8, 128, units).astype(F32), axis=0).astype(BF)
+    summed = jnp.sum(blocks.reshape(8, 2, 64, units).astype(F32), axis=0).astype(BF)
+    summed = jnp.where(x % 2 == 0, summed, summed[::-1]).reshape(128, units)
     gate_late, up_late, summed = lax.optimization_barrier((gate_pre, up_pre, summed))
     gate_f, sigma, act_value, up_f = activation(gate_late, up_late)
     grad_hidden = summed.astype(F32)
     grad_up = (grad_hidden * act_value).astype(BF)
     grad_gate = (grad_hidden * up_f * sigma * (1.0 + gate_f * (1.0 - sigma))).astype(BF)
 
+    out_own, out_other = place_out(jnp.stack([x, core]), pieces)
+    out_own, out_other = out_own.reshape(1024, width), out_other.reshape(1024, width)
     projected = exact(tp_rows(core), out_own) + exact(tp_rows(1 - core), out_other)
     first_moment = 0.9 * first_moment_in + 0.1 * projected
     second_moment = 0.999 * second_moment_in + 0.001 * projected * projected

time: 247 us -> 222 us (0.90)
  waiting for transfers between devices: 69.9 us -> 32 us
  starting transfers between devices: 73.6 us -> 81.3 us
  other arithmetic: 5 us -> 10.1 us
    ppermute x3, waiting for transfers between devices: 42.3 us -> 13.4 us  [along_x(): lax.ppermute(value, ('row', 'col'), [(source, 32 * row + c) for source, (...]
    ppermute x7, waiting for transfers between devices: 10.2 us -> 5.55 us  [along_y(): lax.ppermute(value, TOK, [(index(y, q), index((y + 1 - 2 * q) % 8, q)) fo...]
    ppermute x1 -> x2, starting transfers between devices: 1.91 us -> 5.8 us  [work(): got = lax.ppermute(other, TOK, PAIR)]
    convert_element_type x0 -> x2, other arithmetic: none -> 3.41 us  [work(): (mine.astype(F32) + got.astype(F32)).astype(BF).reshape(8, 64, units)]
    ppermute x5, starting transfers between devices: 19.8 us -> 22.4 us  [work(): lax.ppermute(totals, 'col', [(c, c ^ bit) for c in range(32)])]
    dot_general x3 -> x5, matrix products: 11.4 us -> 10.8 us  [dot_nt(): lax.dot_general(left, right, (((1,), (1,)), ((), ())), preferred_element_...]
  transfers between devices with their start and end apart: 20 -> 21, of which waited for: 12 -> 10; matrix products, arithmetic and copies ran while one was open for 10% -> 14% of each run, Pallas kernels for 3% -> 3%
where the time goes in v2:
time: 222 us; the launch traced here: 221 us
  starting transfers between devices  81.3 us (37%)
  blocking collectives  64.8 us (29%)
  waiting for transfers between devices  32 us (14%)
  matrix products  21.3 us (10%)
  other arithmetic  10.1 us (5%)
  Pallas kernels  7.54 us (3%)
  local copies, waits for them, and re-layouts  2.7 us (1%)
    all_to_all x1, blocking collectives, gather_out(): lax.all_to_all(sent, 'col', 0, 0, tiled=True, axis_index_groups=Z_GROUPS)  38.8 us
    all_gather x1, blocking collectives, work(): basis_all = lax.all_gather(basis, TOK, axis=0, tiled=True)  26 us
    ppermute x7, starting transfers between devices, along_y(): lax.ppermute(value, TOK, [(index(y, q), index((y + 1 - 2 * q) % 8, q)) fo...  23.2 us
    ppermute x5, starting transfers between devices, work(): lax.ppermute(totals, 'col', [(c, c ^ bit) for c in range(32)])  22.4 us
    ppermute x3, waiting for transfers between devices, along_x(): lax.ppermute(value, ('row', 'col'), [(source, 32 * row + c) for source, (...  13.4 us
    dot_general x5, matrix products, dot_nt(): lax.dot_general(left, right, (((1,), (1,)), ((), ())), preferred_element_...  10.8 us
    ppermute x5, waiting for transfers between devices, work(): lax.ppermute(totals, 'col', [(c, c ^ bit) for c in range(32)])  10.1 us
    ppermute x3, starting transfers between devices, along_x(): lax.ppermute(value, ('row', 'col'), [(source, 32 * row + c) for source, (...  9.26 us
  transfers between devices with their start and end apart: 21, of which 10 were waited for; matrix products, arithmetic and copies ran while one was open for 14% of the time, Pallas kernels for 3%

profile of v2, /device:TPU:8, one launch (start us, length us, event | category | flops | bytes accessed | tf_op | source)
XLA Modules:
  0.0 221.0 jit_solution(16065737312210118163)
XLA Ops:
  1.9 38.8 %all_to_all.33.refs_0_ = bf16[8,64,1024]{2,1,0:T(8,128)(2,1)S(1)} all-to-all(bf16[8,64,1024]{2,1,0:T(8,128)(2,1)S(1)} %broadcast_in_dim.4), channel_id=1, replica_groups={{0,4,8,12,16,20,24,28},{1,5,9,13,17,21,25,29},{2,6,10,14,18,22,26,30},{..., dimensions={0} | all-to-all | bytes 2097152 | tf_op jit(solution)/shard_map/all_to_all | solution.py:99
  40.7 3.4 %collective-permute-start = (bf16[8,64,1024]{2,1,0:T(8,128)(2,1)S(1)}, bf16[8,64,1024]{2,1,0:T(8,128)(2,1)}, u32[]{:S(2)}, u32[]{:S(2)}) collective-permute-start(bf16[8,64,1024]{2,1,0:T(8,128)(2,1)S(1)} %all_to_all.33.refs_0_), channel_id=1, source_target_pairs={{0,1},{1,2},{2,3},{3,0},{4,5},{5,6},{6,7},{7,4},{8,9},{9,10},{10,1... | collective-permute-start | bytes 3145736 | tf_op jit(solution)/shard_map/ppermute | solution.py:27
  44.3 3.5 %collective-permute-start.5 = (bf16[128,896]{1,0:T(8,128)(2,1)S(1)}, bf16[128,896]{1,0:T(8,128)(2,1)S(1)}, u32[]{:S(2)}, u32[]{:S(2)}) collective-permute-start(bf16[128,896]{1,0:T(8,128)(2,1)S(1)} %fusion.13.refs_0_), channel_id=1, source_target_pairs={{0,256},{32,480},{256,64},{288,32},{64,320},{96,288},{320,128},{35... | collective-permute-start | bytes 688136 | tf_op jit(solution)/shard_map/ppermute | solution.py:34
  47.8 10.9 %collective-permute-done.refs_1_ = bf16[8,64,1024]{2,1,0:T(8,128)(2,1)} collective-permute-done((bf16[8,64,1024]{2,1,0:T(8,128)(2,1)S(1)}, bf16[8,64,1024]{2,1,0:T(8,128)(2,1)}, u32[]{:S(2)}, u32[]{:S(2)}) %collective-permute-start) | collective-permute-done | bytes 1048608 | tf_op jit(solution)/shard_map/ppermute | solution.py:27
  60.9 3.5 %collective-permute-start.6 = (bf16[128,896]{1,0:T(8,128)(2,1)S(1)}, bf16[128,896]{1,0:T(8,128)(2,1)S(1)}, u32[]{:S(2)}, u32[]{:S(2)}) collective-permute-start(bf16[128,896]{1,0:T(8,128)(2,1)S(1)} %collective-permute-done.5.refs_1_), channel_id=1, source_target_pairs={{0,256},{32,480},{256,64},{288,32},{64,320},{96,288},{320,128},{35... | collective-permute-start | bytes 688136 | tf_op jit(solution)/shard_map/ppermute | solution.py:34
  64.4 4.4 %collective-permute-done.6.refs_2_ = bf16[128,896]{1,0:T(8,128)(2,1)S(1)} collective-permute-done((bf16[128,896]{1,0:T(8,128)(2,1)S(1)}, bf16[128,896]{1,0:T(8,128)(2,1)S(1)}, u32[]{:S(2)}, u32[]{:S(2)}) %collective-permute-start.6) | collective-permute-done | bytes 229408 | tf_op jit(solution)/shard_map/ppermute | solution.py:34
  68.8 3.5 %collective-permute-start.7 = (bf16[128,896]{1,0:T(8,128)(2,1)S(1)}, bf16[128,896]{1,0:T(8,128)(2,1)}, u32[]{:S(2)}, u32[]{:S(2)}) collective-permute-start(bf16[128,896]{1,0:T(8,128)(2,1)S(1)} %collective-permute-done.6.refs_2_), channel_id=1, source_target_pairs={{0,256},{32,480},{256,64},{288,32},{64,320},{96,288},{320,128},{35... | collective-permute-start | bytes 688136 | tf_op jit(solution)/shard_map/ppermute | solution.py:34
  72.3 26.0 %all_gather.3 = bf16[512,896]{1,0:T(8,128)(2,1)S(1)} all-gather(bf16[32,896]{1,0:T(8,128)(2,1)S(1)} %copy-done.16), channel_id=1, replica_groups=mesh['dp'=2,'row'=8,'col'=32] {'dp','row'}, dimensions={0}, use_global_device_ids=true | all-gather | bytes 974848 | tf_op jit(solution)/shard_map/all_gather | solution.py:137
  102.1 4.3 %all-to-all-start.2 = ((bf16[32,16,128]{2,1,0:T(8,128)(2,1)}), bf16[32,16,128]{2,1,0:T(8,128)(2,1)S(1)}, u32[]{:S(2)}, u32[]{:S(2)}) async-start(bf16[32,16,128]{2,1,0:T(8,128)(2,1)} %bitcast.91), calls=%async_computation.2 | async-start | bytes 262144 | tf_op jit(solution)/shard_map/all_to_all | solution.py:139
  106.5 3.9 %collective-permute-start.9 = (bf16[128,896]{1,0:T(8,128)(2,1)}, bf16[128,896]{1,0:T(8,128)(2,1)}, u32[]{:S(2)}, u32[]{:S(2)}) collective-permute-start(bf16[128,896]{1,0:T(8,128)(2,1)} %collective-permute-done.8.refs_4_), channel_id=1, source_target_pairs={{0,256},{32,480},{256,64},{288,32},{64,320},{96,288},{320,128},{35... | collective-permute-start | bytes 688136 | tf_op jit(solution)/shard_map/ppermute | solution.py:34
  110.5 3.7 %collective-permute-start.3 = (bf16[8,64,1024]{2,1,0:T(8,128)(2,1)}, bf16[8,64,1024]{2,1,0:T(8,128)(2,1)S(1)}, u32[]{:S(2)}, u32[]{:S(2)}) collective-permute-start(bf16[8,64,1024]{2,1,0:T(8,128)(2,1)} %collective-permute-done.1.refs_2_), channel_id=1, source_target_pairs={{0,1},{1,2},{2,3},{3,0},{4,5},{5,6},{6,7},{7,4},{8,9},{9,10},{10,1... | collective-permute-start | bytes 3145736 | tf_op jit(solution)/shard_map/ppermute | solution.py:27
  118.4 3.8 %broadcast_select_fusion.1 = (bf16[512,896]{1,0:T(8,128)(2,1)}, bf16[512,896]{1,0:T(8,128)(2,1)}) fusion(bf16[512,896]{1,0:T(8,128)(2,1)S(1)} %convolution_convert_fusion.3, pred[]{:T(512)S(6)} %eq.15, bf16[512,1024]{1,0:T(8,128)(2,1)} %bitcast.1, bf16[896,1024]{1,0:T(8,128)(2,1)S(1)} %copy-done), kind=kOutput, calls=%fused_computation.12 | convolution fusion | flops 940441600 | bytes 5636097 | tf_op jit(solution)/shard_map/dot_general | solution.py:44
  122.2 3.9 %collective-permute-start.2 = (bf16[512,896]{1,0:T(8,128)(2,1)}, bf16[512,896]{1,0:T(8,128)(2,1)}, u32[]{:S(2)}, u32[]{:S(2)}) collective-permute-start(bf16[512,896]{1,0:T(8,128)(2,1)} %get-tuple-element.29), channel_id=1, source_target_pairs={{0,32},{32,0},{64,96},{96,64},{128,160},{160,128},{192,224},{224,1... | collective-permute-start | bytes 2752520 | tf_op jit(solution)/shard_map/ppermute | solution.py:155
  136.7 6.3 %all-to-all-start.3 = ((f32[16,16,128]{2,1,0:T(8,128)}), f32[16,16,128]{2,1,0:T(8,128)S(1)}, u32[]{:S(2)}, u32[]{:S(2)}) async-start(f32[16,16,128]{2,1,0:T(8,128)} %broadcast_in_dim.5), calls=%async_computation.3 | async-start | bytes 262144 | tf_op jit(solution)/shard_map/all_to_all | solution.py:142
  143.0 3.4 %collective-permute-start.11 = (bf16[128,896]{1,0:T(8,128)(2,1)}, bf16[128,896]{1,0:T(8,128)(2,1)}, u32[]{:S(2)}, u32[]{:S(2)}) collective-permute-start(bf16[128,896]{1,0:T(8,128)(2,1)} %collective-permute-done.10.refs_6_), channel_id=1, source_target_pairs={{0,256},{32,480},{256,64},{288,32},{64,320},{96,288},{320,128},{35... | collective-permute-start | bytes 688136 | tf_op jit(solution)/shard_map/ppermute | solution.py:34
  161.4 8.1 %all-to-all-start.1 = ((bf16[8,128,896]{2,1,0:T(8,128)(2,1)}), bf16[8,128,896]{2,1,0:T(8,128)(2,1)}, u32[]{:S(2)}, u32[]{:S(2)}) async-start(bf16[8,128,896]{2,1,0:T(8,128)(2,1)} %bitcast.78), calls=%async_computation.1 | async-start | bytes 3670016 | tf_op jit(solution)/shard_map/all_to_all | solution.py:158
  169.5 4.5 %place_out.1 = (bf16[8,2,64,1024]{3,2,1,0:T(8,128)(2,1)}, bf16[8,2,64,1024]{3,2,1,0:T(8,128)(2,1)}) custom-call(s32[2]{0:T(128)} %pad_add_fusion.1.here_ref, bf16[8,64,1024]{2,1,0:T(8,128)(2,1)} %copy-done.1, bf16[8,64,1024]{2,1,0:T(8,128)(2,1)} %collective-permute-done.refs_1_, bf16[8,64,1024]{2,1,0:T(8,128)(2,1)} %collective-permute-done.1.refs_2_, ...), custom_call_target="tpu_custom_call" | custom-call | tf_op jit(solution)/shard_map/place_out/pallas_call | solution.py:69
  179.9 3.2 %collective-permute-done.13 = f32[2,1024]{1,0:T(2,128)S(1)} collective-permute-done((f32[2,1024]{1,0:T(2,128)S(1)}, f32[2,1024]{1,0:T(2,128)S(1)}, u32[]{:S(2)}, u32[]{:S(2)}) %collective-permute-start.13) | collective-permute-done | bytes 8224 | tf_op jit(solution)/shard_map/ppermute | solution.py:175
  183.1 3.9 %collective-permute-start.14 = (f32[2,1024]{1,0:T(2,128)S(1)}, f32[2,1024]{1,0:T(2,128)S(1)}, u32[]{:S(2)}, u32[]{:S(2)}) collective-permute-start(f32[2,1024]{1,0:T(2,128)S(1)} %fusion.36), channel_id=1, source_target_pairs={{0,2},{1,3},{2,0},{3,1},{4,6},{5,7},{6,4},{7,5},{8,10},{9,11},{10,... | collective-permute-start | bytes 24584 | tf_op jit(solution)/shard_map/ppermute | solution.py:175
  190.2 3.6 %collective-permute-start.15 = (f32[2,1024]{1,0:T(2,128)S(1)}, f32[2,1024]{1,0:T(2,128)S(1)}, u32[]{:S(2)}, u32[]{:S(2)}) collective-permute-start(f32[2,1024]{1,0:T(2,128)S(1)} %fusion.56), channel_id=1, source_target_pairs={{0,4},{1,5},{2,6},{3,7},{4,0},{5,1},{6,2},{7,3},{8,12},{9,13},{10,... | collective-permute-start | bytes 24584 | tf_op jit(solution)/shard_map/ppermute | solution.py:175
  195.7 4.5 %collective-permute-start.16 = (f32[2,1024]{1,0:T(2,128)S(1)}, f32[2,1024]{1,0:T(2,128)S(1)}, u32[]{:S(2)}, u32[]{:S(2)}) collective-permute-start(f32[2,1024]{1,0:T(2,128)S(1)} %add.126), channel_id=1, source_target_pairs={{0,8},{1,9},{2,10},{3,11},{4,12},{5,13},{6,14},{7,15},{8,0},{9,1},... | collective-permute-start | bytes 24584 | tf_op jit(solution)/shard_map/ppermute | solution.py:175
  202.2 8.1 %collective-permute-start.17 = (f32[2,1024]{1,0:T(2,128)S(1)}, f32[2,1024]{1,0:T(2,128)S(1)}, u32[]{:S(2)}, u32[]{:S(2)}) collective-permute-start(f32[2,1024]{1,0:T(2,128)S(1)} %add.127), channel_id=1, source_target_pairs={{0,16},{1,17},{2,18},{3,19},{4,20},{5,21},{6,22},{7,23},{8,24},{9,... | collective-permute-start | bytes 24584 | tf_op jit(solution)/shard_map/ppermute | solution.py:175
  210.3 4.3 %fusion.39 = f32[896,1024]{1,0:T(8,128)S(1)} fusion(bf16[1024,896]{1,0:T(8,128)(2,1)} %collective-permute-done.12, bf16[1024,1024]{1,0:T(8,128)(2,1)} %bitcast.85), kind=kOutput, calls=%fused_computation.77 | convolution fusion | flops 1879048192 | bytes 7602176 | tf_op jit(solution)/shard_map/dot_general | solution.py:48
  214.6 3.5 %multiply_convert_fusion = bf16[896,1024]{1,0:T(8,128)(2,1)} fusion(f32[896,1024]{1,0:T(8,128)S(1)} %fusion.39, f32[1024]{0:T(1024)S(1)} %bitcast.99, bf16[1024,896]{1,0:T(8,128)(2,1)S(1)} %bitcast.87, bf16[1024,1024]{1,0:T(8,128)(2,1)S(1)} %bitcast.83), kind=kOutput, calls=%fused_computation | convolution fusion | flops 1883635712 | bytes 9441280 | tf_op jit(solution)/shard_map/dot_general | solution.py:48
  (90 shorter events, 52.9 us)
Async XLA Ops:
  0.6 113.5 %copy-start = (bf16[896,1024]{1,0:T(8,128)(2,1)S(1)}, bf16[896,1024]{1,0:T(8,128)(2,1)}, u32[]{:S(2)}) copy-start(bf16[896,1024]{1,0:T(8,128)(2,1)} %param.10) | copy-start | bytes 5505028
  0.7 71.6 %copy-start.16 = (bf16[32,896]{1,0:T(8,128)(2,1)S(1)}, bf16[32,896]{1,0:T(8,128)(2,1)}, u32[]{:S(2)}) copy-start(bf16[32,896]{1,0:T(8,128)(2,1)} %param.11) | copy-start | bytes 172036
  40.7 74.8 %copy-start.1 = (bf16[8,64,1024]{2,1,0:T(8,128)(2,1)}, bf16[8,64,1024]{2,1,0:T(8,128)(2,1)S(1)}, u32[]{:S(2)}) copy-start(bf16[8,64,1024]{2,1,0:T(8,128)(2,1)S(1)} %all_to_all.33.refs_0_) | copy-start | bytes 3145732
  40.7 18.0 %collective-permute-start = (bf16[8,64,1024]{2,1,0:T(8,128)(2,1)S(1)}, bf16[8,64,1024]{2,1,0:T(8,128)(2,1)}, u32[]{:S(2)}, u32[]{:S(2)}) collective-permute-start(bf16[8,64,1024]{2,1,0:T(8,128)(2,1)S(1)} %all_to_all.33.refs_0_), channel_id=1, source_target_pairs={{0,1},{1,2},{2,3},{3,0},{4,5},{5,6},{6,7},{7,4},{8,9},{9,10},{10,1... | collective-permute-start | bytes 3145736 | tf_op jit(solution)/shard_map/ppermute | solution.py:27
  44.3 16.6 %collective-permute-start.5 = (bf16[128,896]{1,0:T(8,128)(2,1)S(1)}, bf16[128,896]{1,0:T(8,128)(2,1)S(1)}, u32[]{:S(2)}, u32[]{:S(2)}) collective-permute-start(bf16[128,896]{1,0:T(8,128)(2,1)S(1)} %fusion.13.refs_0_), channel_id=1, source_target_pairs={{0,256},{32,480},{256,64},{288,32},{64,320},{96,288},{320,128},{35... | collective-permute-start | bytes 688136 | tf_op jit(solution)/shard_map/ppermute | solution.py:34
  58.7 51.8 %collective-permute-start.1 = (bf16[8,64,1024]{2,1,0:T(8,128)(2,1)}, bf16[8,64,1024]{2,1,0:T(8,128)(2,1)}, u32[]{:S(2)}, u32[]{:S(2)}) collective-permute-start(bf16[8,64,1024]{2,1,0:T(8,128)(2,1)} %collective-permute-done.refs_1_), channel_id=1, source_target_pairs={{0,1},{1,2},{2,3},{3,0},{4,5},{5,6},{6,7},{7,4},{8,9},{9,10},{10,1... | collective-permute-start | bytes 3145736 | tf_op jit(solution)/shard_map/ppermute | solution.py:27
  60.9 7.9 %collective-permute-start.6 = (bf16[128,896]{1,0:T(8,128)(2,1)S(1)}, bf16[128,896]{1,0:T(8,128)(2,1)S(1)}, u32[]{:S(2)}, u32[]{:S(2)}) collective-permute-start(bf16[128,896]{1,0:T(8,128)(2,1)S(1)} %collective-permute-done.5.refs_1_), channel_id=1, source_target_pairs={{0,256},{32,480},{256,64},{288,32},{64,320},{96,288},{320,128},{35... | collective-permute-start | bytes 688136 | tf_op jit(solution)/shard_map/ppermute | solution.py:34
  68.8 29.5 %collective-permute-start.7 = (bf16[128,896]{1,0:T(8,128)(2,1)S(1)}, bf16[128,896]{1,0:T(8,128)(2,1)}, u32[]{:S(2)}, u32[]{:S(2)}) collective-permute-start(bf16[128,896]{1,0:T(8,128)(2,1)S(1)} %collective-permute-done.6.refs_2_), channel_id=1, source_target_pairs={{0,256},{32,480},{256,64},{288,32},{64,320},{96,288},{320,128},{35... | collective-permute-start | bytes 688136 | tf_op jit(solution)/shard_map/ppermute | solution.py:34
  98.3 8.2 %collective-permute-start.8 = (bf16[128,896]{1,0:T(8,128)(2,1)}, bf16[128,896]{1,0:T(8,128)(2,1)}, u32[]{:S(2)}, u32[]{:S(2)}) collective-permute-start(bf16[128,896]{1,0:T(8,128)(2,1)} %collective-permute-done.7.refs_3_), channel_id=1, source_target_pairs={{0,256},{32,480},{256,64},{288,32},{64,320},{96,288},{320,128},{35... | collective-permute-start | bytes 688136 | tf_op jit(solution)/shard_map/ppermute | solution.py:34
  102.1 33.9 %all-to-all-start.2 = ((bf16[32,16,128]{2,1,0:T(8,128)(2,1)}), bf16[32,16,128]{2,1,0:T(8,128)(2,1)S(1)}, u32[]{:S(2)}, u32[]{:S(2)}) async-start(bf16[32,16,128]{2,1,0:T(8,128)(2,1)} %bitcast.91), calls=%async_computation.2 | async-start | bytes 262144 | tf_op jit(solution)/shard_map/all_to_all | solution.py:139
  106.5 26.5 %collective-permute-start.9 = (bf16[128,896]{1,0:T(8,128)(2,1)}, bf16[128,896]{1,0:T(8,128)(2,1)}, u32[]{:S(2)}, u32[]{:S(2)}) collective-permute-start(bf16[128,896]{1,0:T(8,128)(2,1)} %collective-permute-done.8.refs_4_), channel_id=1, source_target_pairs={{0,256},{32,480},{256,64},{288,32},{64,320},{96,288},{320,128},{35... | collective-permute-start | bytes 688136 | tf_op jit(solution)/shard_map/ppermute | solution.py:34
  110.5 18.1 %collective-permute-start.3 = (bf16[8,64,1024]{2,1,0:T(8,128)(2,1)}, bf16[8,64,1024]{2,1,0:T(8,128)(2,1)S(1)}, u32[]{:S(2)}, u32[]{:S(2)}) collective-permute-start(bf16[8,64,1024]{2,1,0:T(8,128)(2,1)} %collective-permute-done.1.refs_2_), channel_id=1, source_target_pairs={{0,1},{1,2},{2,3},{3,0},{4,5},{5,6},{6,7},{7,4},{8,9},{9,10},{10,1... | collective-permute-start | bytes 3145736 | tf_op jit(solution)/shard_map/ppermute | solution.py:27
  122.2 34.3 %collective-permute-start.2 = (bf16[512,896]{1,0:T(8,128)(2,1)}, bf16[512,896]{1,0:T(8,128)(2,1)}, u32[]{:S(2)}, u32[]{:S(2)}) collective-permute-start(bf16[512,896]{1,0:T(8,128)(2,1)} %get-tuple-element.29), channel_id=1, source_target_pairs={{0,32},{32,0},{64,96},{96,64},{128,160},{160,128},{192,224},{224,1... | collective-permute-start | bytes 2752520 | tf_op jit(solution)/shard_map/ppermute | solution.py:155
  131.1 27.3 %collective-permute-start.4 = (bf16[512,896]{1,0:T(8,128)(2,1)}, bf16[512,896]{1,0:T(8,128)(2,1)}, u32[]{:S(2)}, u32[]{:S(2)}) collective-permute-start(bf16[512,896]{1,0:T(8,128)(2,1)} %get-tuple-element.27), channel_id=1, source_target_pairs={{0,32},{32,0},{64,96},{96,64},{128,160},{160,128},{192,224},{224,1... | collective-permute-start | bytes 2752520 | tf_op jit(solution)/shard_map/ppermute | solution.py:155
  133.0 10.0 %collective-permute-start.10 = (bf16[128,896]{1,0:T(8,128)(2,1)}, bf16[128,896]{1,0:T(8,128)(2,1)}, u32[]{:S(2)}, u32[]{:S(2)}) collective-permute-start(bf16[128,896]{1,0:T(8,128)(2,1)} %collective-permute-done.9.refs_5_), channel_id=1, source_target_pairs={{0,256},{32,480},{256,64},{288,32},{64,320},{96,288},{320,128},{35... | collective-permute-start | bytes 688136 | tf_op jit(solution)/shard_map/ppermute | solution.py:34
  136.7 13.8 %all-to-all-start.3 = ((f32[16,16,128]{2,1,0:T(8,128)}), f32[16,16,128]{2,1,0:T(8,128)S(1)}, u32[]{:S(2)}, u32[]{:S(2)}) async-start(f32[16,16,128]{2,1,0:T(8,128)} %broadcast_in_dim.5), calls=%async_computation.3 | async-start | bytes 262144 | tf_op jit(solution)/shard_map/all_to_all | solution.py:142
  143.0 8.5 %collective-permute-start.11 = (bf16[128,896]{1,0:T(8,128)(2,1)}, bf16[128,896]{1,0:T(8,128)(2,1)}, u32[]{:S(2)}, u32[]{:S(2)}) collective-permute-start(bf16[128,896]{1,0:T(8,128)(2,1)} %collective-permute-done.10.refs_6_), channel_id=1, source_target_pairs={{0,256},{32,480},{256,64},{288,32},{64,320},{96,288},{320,128},{35... | collective-permute-start | bytes 688136 | tf_op jit(solution)/shard_map/ppermute | solution.py:34
  154.5 55.7 %collective-permute-start.12 = (bf16[1024,896]{1,0:T(8,128)(2,1)}, bf16[1024,896]{1,0:T(8,128)(2,1)}, u32[]{:S(2)}, u32[]{:S(2)}) collective-permute-start(bf16[1024,896]{1,0:T(8,128)(2,1)} %bitcast.86), channel_id=1, source_target_pairs={{0,32},{32,0},{64,96},{96,64},{128,160},{160,128},{192,224},{224,1... | collective-permute-start | bytes 5505032 | tf_op jit(solution)/shard_map/ppermute | solution.py:135
  161.4 56.7 %all-to-all-start.1 = ((bf16[8,128,896]{2,1,0:T(8,128)(2,1)}), bf16[8,128,896]{2,1,0:T(8,128)(2,1)}, u32[]{:S(2)}, u32[]{:S(2)}) async-start(bf16[8,128,896]{2,1,0:T(8,128)(2,1)} %bitcast.78), calls=%async_computation.1 | async-start | bytes 3670016 | tf_op jit(solution)/shard_map/all_to_all | solution.py:158
  177.6 5.5 %collective-permute-start.13 = (f32[2,1024]{1,0:T(2,128)S(1)}, f32[2,1024]{1,0:T(2,128)S(1)}, u32[]{:S(2)}, u32[]{:S(2)}) collective-permute-start(f32[2,1024]{1,0:T(2,128)S(1)} %pad_maximum_fusion.1), channel_id=1, source_target_pairs={{0,1},{1,0},{2,3},{3,2},{4,5},{5,4},{6,7},{7,6},{8,9},{9,8},{10,11... | collective-permute-start | bytes 24584 | tf_op jit(solution)/shard_map/ppermute | solution.py:175
  183.1 7.0 %collective-permute-start.14 = (f32[2,1024]{1,0:T(2,128)S(1)}, f32[2,1024]{1,0:T(2,128)S(1)}, u32[]{:S(2)}, u32[]{:S(2)}) collective-permute-start(f32[2,1024]{1,0:T(2,128)S(1)} %fusion.36), channel_id=1, source_target_pairs={{0,2},{1,3},{2,0},{3,1},{4,6},{5,7},{6,4},{7,5},{8,10},{9,11},{10,... | collective-permute-start | bytes 24584 | tf_op jit(solution)/shard_map/ppermute | solution.py:175
  190.2 5.5 %collective-permute-start.15 = (f32[2,1024]{1,0:T(2,128)S(1)}, f32[2,1024]{1,0:T(2,128)S(1)}, u32[]{:S(2)}, u32[]{:S(2)}) collective-permute-start(f32[2,1024]{1,0:T(2,128)S(1)} %fusion.56), channel_id=1, source_target_pairs={{0,4},{1,5},{2,6},{3,7},{4,0},{5,1},{6,2},{7,3},{8,12},{9,13},{10,... | collective-permute-start | bytes 24584 | tf_op jit(solution)/shard_map/ppermute | solution.py:175
  195.7 6.4 %collective-permute-start.16 = (f32[2,1024]{1,0:T(2,128)S(1)}, f32[2,1024]{1,0:T(2,128)S(1)}, u32[]{:S(2)}, u32[]{:S(2)}) collective-permute-start(f32[2,1024]{1,0:T(2,128)S(1)} %add.126), channel_id=1, source_target_pairs={{0,8},{1,9},{2,10},{3,11},{4,12},{5,13},{6,14},{7,15},{8,0},{9,1},... | collective-permute-start | bytes 24584 | tf_op jit(solution)/shard_map/ppermute | solution.py:175
  202.2 12.3 %collective-permute-start.17 = (f32[2,1024]{1,0:T(2,128)S(1)}, f32[2,1024]{1,0:T(2,128)S(1)}, u32[]{:S(2)}, u32[]{:S(2)}) collective-permute-start(f32[2,1024]{1,0:T(2,128)S(1)} %add.127), channel_id=1, source_target_pairs={{0,16},{1,17},{2,18},{3,19},{4,20},{5,21},{6,22},{7,23},{8,24},{9,... | collective-permute-start | bytes 24584 | tf_op jit(solution)/shard_map/ppermute | solution.py:175
  (14 other events, 266.7 us)
